TPU v7x, 128 devices: a whole 4x4x4 slice. The times are simulated.
128 devices in a mesh: pb: 8 (over z_hi, x), ka: 16 (over z_lo, y, core).
Axes of the slice: x: 4, y: 4, z: 4 (z_hi: 2, z_lo: 2; z = z_hi * 2 + z_lo), core: 2. Of those that a mesh axis runs over, the one named last changes fastest.
Arguments:
- feat_first: bfloat16 [32768, 128], P(('pb', 'ka')), may hold values from -16 to 16
- feat_second: bfloat16 [32768, 128], P(('ka', 'pb')), may hold values from -18 to 18
- value_weight: bfloat16 [128, 128], replicated, may hold values from -0.5 to 0.5
- out_weight: bfloat16 [128, 128], replicated, may hold values from -0.5 to 0.5
- conv_weight: bfloat16 [3, 3, 128, 128], replicated, may hold values from -0.1875 to 0.1875
- conv_bias: bfloat16 [128], replicated, may hold values from -3 to 3
Outputs:
- refined: bfloat16 [128, 256, 128], P(('pb', 'ka'))
All inputs are finite; a program needn't handle non-finite values.
Results may differ from a plain program's by a relative error of at most 0.0055.
Values may be sent and summed in bfloat16 or wider, within the bound.
No kernel may reach another device: no remote copies, remote signals or barrier semaphores. Data moves between devices by JAX's collectives and lax.ppermute only.
A program may use at most 192 MiB of HBM per device.

v0:
```python
import functools

import jax
import jax.numpy as jnp
from jax import lax
from jax.experimental import pallas as pl
from jax.experimental.pallas import tpu as pltpu
from jax.sharding import PartitionSpec as P


AXES = ("pb", "ka")
SIZES = dict(zh=2, x=4, zl=2, y=4, c=2)
LOG2E = 1.4426950408889634
VMEM = pl.BlockSpec(memory_space=pltpu.VMEM)
NT = (((1,), (1,)), ((), ()))
ROWS = 128
CHUNK = 512


def place(index):
    at = {}
    for name in reversed(SIZES):
        index, at[name] = divmod(index, SIZES[name])
    at["z"] = at["zh"] * 2 + at["zl"]
    return at


def number(at):
    at = dict(at)
    at["zh"], at["zl"] = divmod(at["z"], 2)
    index = 0
    for name, size in SIZES.items():
        index = index * size + at[name]
    return index


def trade(block, kind, *names):
    pairs = []
    for source in range(128):
        at = place(source)
        name = names[at["c"] % len(names)]
        at[name] = dict(A=at[name] ^ 1, B=3 - at[name], AB=at[name] ^ 2)[kind]
        pairs.append((source, number(at)))
    return lax.ppermute(block, AXES, pairs)


def swap(block):
    return lax.ppermute(block, AXES, [(i, i ^ 1) for i in range(128)])


def params():
    return pltpu.CompilerParams(vmem_limit_bytes=48 << 20)


def cost(rows, keys):
    scores = rows * keys
    return pl.CostEstimate(flops=scores * 768, transcendentals=scores, bytes_accessed=1 << 20)


def attend(queries, pieces, state, scale):
    ones = jnp.ones((CHUNK, 128), jnp.bfloat16)
    state = list(state)
    for keys_ref in pieces:
        for at in range(0, keys_ref.shape[0], CHUNK):
            k = keys_ref[at : at + CHUNK]
            v = jnp.concatenate([k, ones], axis=1)
            for b, q in enumerate(queries):
                s = lax.dot_general(q[...], k, NT, preferred_element_type=jnp.float32)
                new = jnp.broadcast_to(jnp.max(s, axis=1, keepdims=True), (ROWS, 128))
                if state[b] is not None:
                    new = jnp.maximum(state[b][0], new)
                all_new = jnp.concatenate([new] * (CHUNK // 128), axis=1)
                p = jnp.exp2(((s - all_new) * scale).astype(jnp.bfloat16))
                weighted = jnp.dot(p, v, preferred_element_type=jnp.float32)
                if state[b] is not None:
                    decay = jnp.exp2((state[b][0] - new) * scale)
                    weighted = state[b][1] * jnp.concatenate([decay, decay], axis=1) + weighted
                state[b] = (new, weighted)
    return state


def blocks_of(refs):
    return [ref.at[pl.ds(at, ROWS)] for ref in refs for at in range(0, ref.shape[0], ROWS)]


def keys_kernel(scale, nq, nk, started, row, *refs):
    refs = list(refs)
    take = lambda n: [refs.pop(0) for _ in range(n)]
    queries, pieces = blocks_of(take(nq)), take(nk)
    state = [None] * len(queries)
    if started:
        peaks, sums = blocks_of(take(1)), blocks_of(take(1))
        first = row // ROWS
        state = [(peaks[first + b][...], sums[first + b][...]) for b in range(len(queries))]
    peaks, sums = blocks_of(refs[:1]), blocks_of(refs[1:])
    for b, (peak, weighted) in enumerate(attend(queries, pieces, state, scale)):
        peaks[b][...] = peak
        sums[b][...] = weighted


def keys_call(queries, pieces, scale, state=(), row=0):
    rows = sum(q.shape[0] for q in queries)
    return pl.pallas_call(
        functools.partial(keys_kernel, scale, len(queries), len(pieces), bool(state), row),
        out_shape=[
            jax.ShapeDtypeStruct((rows, 128), jnp.float32),
            jax.ShapeDtypeStruct((rows, 256), jnp.float32),
        ],
        in_specs=[VMEM] * (len(queries) + len(pieces) + len(state)),
        out_specs=[VMEM] * 2,
        compiler_params=params(),
        cost_estimate=cost(rows, sum(p.shape[0] for p in pieces)),
        name="keys",
    )(*queries, *pieces, *state)


def split3(x):
    high = x.astype(jnp.bfloat16)
    rest = x - high.astype(jnp.float32)
    mid = rest.astype(jnp.bfloat16)
    low = (rest - mid.astype(jnp.float32)).astype(jnp.bfloat16)
    return high.astype(jnp.float32), mid.astype(jnp.float32), low.astype(jnp.float32)


def pack(level, weighted, out_ref):
    mass = weighted[:, 128:]
    out_ref[0:256] = (weighted[:, :128] / mass).astype(jnp.bfloat16)
    rows = jnp.transpose(level + jnp.log2(mass))[0:8]
    left, right = split3(rows[:, :128]), split3(rows[:, 128:])
    at = lax.broadcasted_iota(jnp.int32, (8, 128), 0)
    tile = jnp.where(at == 0, left[0], 0.0)
    for r, part in enumerate((left[1], left[2], right[0], right[1], right[2])):
        tile = jnp.where(at == r + 1, part, tile)
    out_ref[256:272] = jnp.concatenate([tile, tile], axis=0).astype(jnp.bfloat16)


def absorb(level, weighted, part_ref):
    tile = part_ref[256:272].astype(jnp.float32)
    left = tile[0:1] + tile[1:2] + tile[2:3]
    right = tile[3:4] + tile[4:5] + tile[5:6]
    row = jnp.concatenate([left, right], axis=1)
    other = jnp.transpose(jnp.broadcast_to(row, (128, 256)))
    top = jnp.maximum(level, other)
    mine, theirs = jnp.exp2(level - top), jnp.exp2(other - top)
    both = part_ref[0:256].astype(jnp.float32) * theirs
    weighted = jnp.concatenate(
        [weighted[:, :128] * mine + both, weighted[:, 128:] * mine + theirs], axis=1
    )
    return top, weighted


def last_kernel(scale, row, nk, packed, *refs):
    refs = list(refs)
    q_ref, peak_ref, sum_ref = refs[:3]
    pieces, refs = refs[3 : 3 + nk], refs[3 + nk :]
    outs = refs[-1:] if packed else refs[-2:]
    arrived = refs[: len(refs) - len(outs)]
    queries = blocks_of([q_ref])
    state = [
        (peak_ref[row + at : row + at + ROWS], sum_ref[row + at : row + at + ROWS])
        for at in range(0, 256, ROWS)
    ]
    state = attend(queries, pieces, state, scale)
    level = jnp.concatenate([peak for peak, _ in state], axis=0) * scale
    weighted = jnp.concatenate([total for _, total in state], axis=0)
    for part in arrived:
        level, weighted = absorb(level, weighted, part)
    if packed:
        pack(level, weighted, outs[0])
    else:
        outs[0][...] = level
        outs[1][...] = weighted


def last_call(query, row, state, pieces, scale, arrived=(), packed=True):
    shapes = jax.ShapeDtypeStruct((272, 128), jnp.bfloat16)
    if not packed:
        shapes = [
            jax.ShapeDtypeStruct((256, 128), jnp.float32),
            jax.ShapeDtypeStruct((256, 256), jnp.float32),
        ]
    return pl.pallas_call(
        functools.partial(last_kernel, scale, row, len(pieces), packed),
        out_shape=shapes,
        in_specs=[VMEM] * (3 + len(pieces) + len(arrived)),
        out_specs=VMEM if packed else [VMEM] * 2,
        compiler_params=params(),
        cost_estimate=cost(256, sum(p.shape[0] for p in pieces)),
        name="last_keys",
    )(query, *state, *pieces, *arrived)


def merge_kernel(q_ref, vw_ref, ow_ref, level_ref, sum_ref, *refs):
    parts, out_ref = refs[:-1], refs[-1]
    level, weighted = level_ref[...], sum_ref[...]
    for part in parts:
        level, weighted = absorb(level, weighted, part)
    mean = (weighted[:, :128] / weighted[:, 128:]).astype(jnp.bfloat16)
    message = jnp.dot(mean, vw_ref[...], preferred_element_type=jnp.float32)
    mixed = q_ref[...].astype(jnp.float32) + jnp.dot(
        message.astype(jnp.bfloat16), ow_ref[...], preferred_element_type=jnp.float32
    )
    out_ref[...] = mixed.astype(jnp.bfloat16)


def merge_call(query, vw, ow, own, parts):
    return pl.pallas_call(
        merge_kernel,
        out_shape=jax.ShapeDtypeStruct((256, 128), jnp.bfloat16),
        in_specs=[VMEM] * (5 + len(parts)),
        out_specs=VMEM,
        compiler_params=params(),
        name="merge",
    )(query, vw, ow, *own, *parts)


def conv_kernel(outer_ref, here_ref, sibling_ref, w_ref, bias_ref, out_ref):
    odd = lax.axis_index("ka") % 2
    total = jnp.zeros((256, 384), jnp.float32)
    for row, a in ((outer_ref, 2 * odd), (here_ref, 1), (sibling_ref, 2 - 2 * odd)):
        taps = jnp.concatenate([w_ref[a, b] for b in range(3)], axis=1)
        total = total + jnp.dot(row[...], taps, preferred_element_type=jnp.float32)
    at = lax.broadcasted_iota(jnp.int32, (256, 128), 0)
    left = jnp.where(at == 0, 0.0, pltpu.roll(total[:, 0:128], 1, 0))
    right = jnp.where(at == 255, 0.0, pltpu.roll(total[:, 256:384], 255, 0))
    conv = left + total[:, 128:256] + right + bias_ref[...].astype(jnp.float32)
    out_ref[...] = (here_ref[...].astype(jnp.float32) + jax.nn.gelu(conv)).astype(jnp.bfloat16)


def conv_call(outer, here, sibling, w, bias):
    return pl.pallas_call(
        conv_kernel,
        out_shape=jax.ShapeDtypeStruct((256, 128), jnp.bfloat16),
        in_specs=[VMEM] * 5,
        out_specs=VMEM,
        compiler_params=params(),
        name="refine",
    )(outer, here, sibling, w, bias.reshape(1, 128))


def local(feat_first, feat_second, value_weight, out_weight, conv_weight, conv_bias):
    scale = feat_first.shape[1] ** -0.5 * LOG2E
    fence = lax.optimization_barrier
    near = [trade(feat_second, kind, "x", "z") for kind in ("AB", "A", "B")]
    queries = [trade(feat_first, kind, "y") for kind in ("AB", "A", "B")]
    mine = jnp.concatenate([feat_second] + near, axis=0)
    far_ab, far_a, far_b = [trade(mine, kind, "z", "x") for kind in ("AB", "A", "B")]
    twin = swap(mine)
    query_ab, query_a, query_b = queries
    queries = [feat_first, query_a, query_b, query_ab]
    state = keys_call(queries, [mine], scale)
    twin, state = fence((twin, state))
    state = keys_call(queries, [twin], scale, state)
    far_a, far_b, state = fence((far_a, far_b, state))
    twin_a, twin_b = swap(far_a), swap(far_b)
    other = keys_call(queries[1:], [far_a, far_b], scale, state, 256)
    far_ab, other = fence((far_ab, other))
    twin_ab = swap(far_ab)
    away = keys_call(queries[2:], [twin_a, twin_b], scale, other, 256)
    twin_ab, away = fence((twin_ab, away))
    tail = [far_ab, twin_ab]
    across = last_call(query_ab, 256, away, tail, scale)
    across = trade(across, "B", "y")
    from_b = last_call(query_b, 0, away, tail, scale)
    from_b = trade(from_b, "B", "y")
    from_a = last_call(query_a, 0, other, [twin_a, twin_b] + tail, scale, (across,))
    from_a = trade(from_a, "A", "y")
    own = last_call(
        feat_first, 0, state, [far_a, far_b, twin_a, twin_b] + tail, scale, packed=False
    )
    mixed = merge_call(feat_first, value_weight, out_weight, own, (from_b, from_a))
    sibling = swap(mixed)
    pairs = [(i, i - 2 if i % 2 else i + 2) for i in range(128)]
    outer = lax.ppermute(sibling, AXES, [p for p in pairs if 0 <= p[1] < 128])
    refined = conv_call(outer, mixed, sibling, conv_weight, conv_bias)
    return refined.reshape(1, 256, 128)


def solution(mesh):
    in_specs = (P(("pb", "ka"), None), P(("ka", "pb"), None), P(), P(), P(), P())
    out_specs = P(("pb", "ka"), None, None)
    return jax.shard_map(local, mesh=mesh, in_specs=in_specs, out_specs=out_specs, check_vma=False)
```

profile of v0, /device:TPU:6, one launch (start us, length us, event | category | flops | bytes accessed | tf_op | source)
XLA Modules:
  0.0 56.1 jit_solution(13487546516936910510)
XLA Ops:
  0.0 1.4 %collective-permute-start = (bf16[256,128]{1,0:T(8,128)(2,1)}, bf16[256,128]{1,0:T(8,128)(2,1)S(1)}, u32[]{:S(2)}, u32[]{:S(2)}) collective-permute-start(bf16[256,128]{1,0:T(8,128)(2,1)} %param.7), channel_id=1, source_target_pairs={{0,32},{1,65},{2,34},{3,67},{4,36},{5,69},{6,38},{7,71},{8,40},{9,... | collective-permute-start | bytes 196616 | tf_op jit(solution)/shard_map/ppermute | solution.py:44
  1.4 2.7 %collective-permute-start.2 = (bf16[256,128]{1,0:T(8,128)(2,1)}, bf16[256,128]{1,0:T(8,128)(2,1)S(1)}, u32[]{:S(2)}, u32[]{:S(2)}) collective-permute-start(bf16[256,128]{1,0:T(8,128)(2,1)} %param.7), channel_id=1, source_target_pairs={{0,48},{1,73},{2,50},{3,75},{4,52},{5,77},{6,54},{7,79},{8,56},{9,... | collective-permute-start | bytes 196616 | tf_op jit(solution)/shard_map/ppermute | solution.py:44
  5.0 1.0 %collective-permute-done = bf16[256,128]{1,0:T(8,128)(2,1)S(1)} collective-permute-done((bf16[256,128]{1,0:T(8,128)(2,1)}, bf16[256,128]{1,0:T(8,128)(2,1)S(1)}, u32[]{:S(2)}, u32[]{:S(2)}) %collective-permute-start) | collective-permute-done | bytes 65568 | tf_op jit(solution)/shard_map/ppermute | solution.py:44
  6.0 1.1 %collective-permute-done.2 = bf16[256,128]{1,0:T(8,128)(2,1)S(1)} collective-permute-done((bf16[256,128]{1,0:T(8,128)(2,1)}, bf16[256,128]{1,0:T(8,128)(2,1)S(1)}, u32[]{:S(2)}, u32[]{:S(2)}) %collective-permute-start.2) | collective-permute-done | bytes 65568 | tf_op jit(solution)/shard_map/ppermute | solution.py:44
  7.1 1.7 %collective-permute-start.8 = (bf16[1024,128]{1,0:T(8,128)(2,1)S(1)}, bf16[1024,128]{1,0:T(8,128)(2,1)S(1)}, u32[]{:S(2)}, u32[]{:S(2)}) collective-permute-start(bf16[1024,128]{1,0:T(8,128)(2,1)S(1)} %constant_dynamic-update-slice_fusion.refs_4_), channel_id=1, source_target_pairs={{0,1},{1,0},{2,3},{3,2},{4,5},{5,4},{6,7},{7,6},{8,9},{9,8},{10,11... | collective-permute-start | bytes 786440 | tf_op jit(solution)/shard_map/ppermute | solution.py:48
  8.8 3.0 %collective-permute-start.6 = (bf16[256,128]{1,0:T(8,128)(2,1)S(1)}, bf16[256,128]{1,0:T(8,128)(2,1)S(1)}, u32[]{:S(2)}, u32[]{:S(2)}) collective-permute-start(bf16[256,128]{1,0:T(8,128)(2,1)S(1)} %copy-done.1), channel_id=1, source_target_pairs={{0,6},{1,7},{2,4},{3,5},{4,2},{5,3},{6,0},{7,1},{8,14},{9,15},{10,... | collective-permute-start | bytes 196616 | tf_op jit(solution)/shard_map/ppermute | solution.py:44
  12.2 2.5 %collective-permute-start.4 = (bf16[1024,128]{1,0:T(8,128)(2,1)S(1)}, bf16[1024,128]{1,0:T(8,128)(2,1)S(1)}, u32[]{:S(2)}, u32[]{:S(2)}) collective-permute-start(bf16[1024,128]{1,0:T(8,128)(2,1)S(1)} %constant_dynamic-update-slice_fusion.refs_4_), channel_id=1, source_target_pairs={{0,72},{1,49},{2,74},{3,51},{4,76},{5,53},{6,78},{7,55},{8,64},{9,... | collective-permute-start | bytes 786440 | tf_op jit(solution)/shard_map/ppermute | solution.py:44
  15.8 4.7 %collective-permute-done.7.refs_3_.refs_2_.refs_1_.refs_0_ = bf16[256,128]{1,0:T(8,128)(2,1)S(1)} collective-permute-done((bf16[256,128]{1,0:T(8,128)(2,1)S(1)}, bf16[256,128]{1,0:T(8,128)(2,1)S(1)}, u32[]{:S(2)}, u32[]{:S(2)}) %collective-permute-start.7) | collective-permute-done | bytes 65568 | tf_op jit(solution)/shard_map/ppermute | solution.py:44
  20.5 1.9 %collective-permute-start.11 = (bf16[1024,128]{1,0:T(8,128)(2,1)S(1)}, bf16[1024,128]{1,0:T(8,128)(2,1)S(1)}, u32[]{:S(2)}, u32[]{:S(2)}) collective-permute-start(bf16[1024,128]{1,0:T(8,128)(2,1)S(1)} %constant_dynamic-update-slice_fusion.refs_4_), channel_id=1, source_target_pairs={{0,64},{1,33},{2,66},{3,35},{4,68},{5,37},{6,70},{7,39},{8,72},{9,... | collective-permute-start | bytes 786440 | tf_op jit(solution)/shard_map/ppermute | solution.py:44
  22.4 1.6 %keys.4 = (f32[1024,128]{1,0:T(8,128)S(1)}, f32[1024,256]{1,0:T(8,128)S(1)}) custom-call(bf16[256,128]{1,0:T(8,128)(2,1)S(1)} %copy-done.1, bf16[256,128]{1,0:T(8,128)(2,1)S(1)} %collective-permute-done.5.refs_1_.refs_0_, bf16[256,128]{1,0:T(8,128)(2,1)S(1)} %collective-permute-done.6.refs_2_.refs_1_.refs_0_, ...), custom_call_target="tpu_custom_call" | custom-call | flops 805306368 | bytes 1048576 | tf_op jit(solution)/shard_map/keys/pallas_call | solution.py:103
  24.0 1.7 %keys.5 = (f32[1024,128]{1,0:T(8,128)S(1)}, f32[1024,256]{1,0:T(8,128)S(1)}) custom-call(bf16[256,128]{1,0:T(8,128)(2,1)S(1)} %copy-done.1, bf16[256,128]{1,0:T(8,128)(2,1)S(1)} %collective-permute-done.5.refs_1_.refs_0_, bf16[256,128]{1,0:T(8,128)(2,1)S(1)} %collective-permute-done.6.refs_2_.refs_1_.refs_0_, ...), custom_call_target="tpu_custom_call" | custom-call | flops 805306368 | bytes 1048576 | tf_op jit(solution)/shard_map/keys/pallas_call | solution.py:103
  26.4 2.4 %keys.6 = (f32[768,128]{1,0:T(8,128)S(1)}, f32[768,256]{1,0:T(8,128)S(1)}) custom-call(bf16[256,128]{1,0:T(8,128)(2,1)S(1)} %collective-permute-done.5.refs_1_.refs_0_, bf16[256,128]{1,0:T(8,128)(2,1)S(1)} %collective-permute-done.6.refs_2_.refs_1_.refs_0_, bf16[256,128]{1,0:T(8,128)(2,1)S(1)} %collective-permute-done.7.refs_3_.refs_2_.refs_1_.refs_0_, ...), custom_call_target="tpu_custom_call" | custom-call | flops 1207959552 | bytes 1048576 | tf_op jit(solution)/shard_map/keys/pallas_call | solution.py:103
  28.9 1.7 %keys.7 = (f32[512,128]{1,0:T(8,128)S(1)}, f32[512,256]{1,0:T(8,128)S(1)}) custom-call(bf16[256,128]{1,0:T(8,128)(2,1)S(1)} %collective-permute-done.6.refs_2_.refs_1_.refs_0_, bf16[256,128]{1,0:T(8,128)(2,1)S(1)} %collective-permute-done.7.refs_3_.refs_2_.refs_1_.refs_0_, bf16[1024,128]{1,0:T(8,128)(2,1)S(1)} %collective-permute-done.9.refs_2_.refs_5_.refs_3_, ...), custom_call_target="tpu_custom_call" | custom-call | flops 805306368 | bytes 1048576 | tf_op jit(solution)/shard_map/keys/pallas_call | solution.py:103
  30.7 1.1 %last_keys.6 = bf16[272,128]{1,0:T(8,128)(2,1)S(1)} custom-call(bf16[256,128]{1,0:T(8,128)(2,1)S(1)} %collective-permute-done.7.refs_3_.refs_2_.refs_1_.refs_0_, f32[512,128]{1,0:T(8,128)S(1)} %get-tuple-element.49.refs_1_, f32[512,256]{1,0:T(8,128)S(1)} %get-tuple-element.50.refs_2_, bf16[1024,128]{1,0:T(8,128)(2,1)S(1)} %collective-permute-done.11.refs_7_.refs_3_.refs_5_, ...), custom_call_target="tpu_custom_call" | custom-call | flops 402653184 | bytes 1048576 | tf_op jit(solution)/shard_map/last_keys/pallas_call | solution.py:182
  32.2 1.1 %last_keys.5 = bf16[272,128]{1,0:T(8,128)(2,1)S(1)} custom-call(bf16[256,128]{1,0:T(8,128)(2,1)S(1)} %collective-permute-done.6.refs_2_.refs_1_.refs_0_, f32[512,128]{1,0:T(8,128)S(1)} %get-tuple-element.49.refs_1_, f32[512,256]{1,0:T(8,128)S(1)} %get-tuple-element.50.refs_2_, bf16[1024,128]{1,0:T(8,128)(2,1)S(1)} %collective-permute-done.11.refs_7_.refs_3_.refs_5_, ...), custom_call_target="tpu_custom_call" | custom-call | flops 402653184 | bytes 1048576 | tf_op jit(solution)/shard_map/last_keys/pallas_call | solution.py:182
  33.3 3.1 %collective-permute-start.13 = (bf16[272,128]{1,0:T(8,128)(2,1)S(1)}, bf16[272,128]{1,0:T(8,128)(2,1)S(1)}, u32[]{:S(2)}, u32[]{:S(2)}) collective-permute-start(bf16[272,128]{1,0:T(8,128)(2,1)S(1)} %last_keys.5), channel_id=1, source_target_pairs={{0,6},{1,7},{2,4},{3,5},{4,2},{5,3},{6,0},{7,1},{8,14},{9,15},{10,... | collective-permute-start | bytes 208904 | tf_op jit(solution)/shard_map/ppermute | solution.py:44
  36.3 1.7 %collective-permute-done.14.refs_7_ = bf16[272,128]{1,0:T(8,128)(2,1)S(1)} collective-permute-done((bf16[272,128]{1,0:T(8,128)(2,1)S(1)}, bf16[272,128]{1,0:T(8,128)(2,1)S(1)}, u32[]{:S(2)}, u32[]{:S(2)}) %collective-permute-start.14) | collective-permute-done | bytes 69664 | tf_op jit(solution)/shard_map/ppermute | solution.py:44
  38.0 1.7 %last_keys.7 = bf16[272,128]{1,0:T(8,128)(2,1)S(1)} custom-call(bf16[256,128]{1,0:T(8,128)(2,1)S(1)} %collective-permute-done.5.refs_1_.refs_0_, f32[768,128]{1,0:T(8,128)S(1)} %get-tuple-element.42.refs_4_.refs_1_, f32[768,256]{1,0:T(8,128)S(1)} %get-tuple-element.43.refs_5_.refs_2_, bf16[1024,128]{1,0:T(8,128)(2,1)S(1)} %collective-permute-done.9.refs_2_.refs_5_.refs_3_, ...), custom_call_target="tpu_custom_call" | custom-call | flops 805306368 | bytes 1048576 | tf_op jit(solution)/shard_map/last_keys/pallas_call | solution.py:182
  39.9 2.4 %last_keys.4 = (f32[256,128]{1,0:T(8,128)S(1)}, f32[256,256]{1,0:T(8,128)S(1)}) custom-call(bf16[256,128]{1,0:T(8,128)(2,1)S(1)} %copy-done.1, f32[1024,128]{1,0:T(8,128)S(1)} %get-tuple-element.35.refs_5_.refs_1_, f32[1024,256]{1,0:T(8,128)S(1)} %get-tuple-element.36.refs_6_.refs_2_, bf16[1024,128]{1,0:T(8,128)(2,1)S(1)} %collective-permute-done.3.refs_3_, ...), custom_call_target="tpu_custom_call" | custom-call | flops 1207959552 | bytes 1048576 | tf_op jit(solution)/shard_map/last_keys/pallas_call | solution.py:182
  42.2 1.9 %collective-permute-done.15.refs_1_ = bf16[272,128]{1,0:T(8,128)(2,1)S(1)} collective-permute-done((bf16[272,128]{1,0:T(8,128)(2,1)S(1)}, bf16[272,128]{1,0:T(8,128)(2,1)S(1)}, u32[]{:S(2)}, u32[]{:S(2)}) %collective-permute-start.15) | collective-permute-done | bytes 69664 | tf_op jit(solution)/shard_map/ppermute | solution.py:44
  44.7 1.2 %collective-permute-done.16.sibling_ref = bf16[256,128]{1,0:T(8,128)(2,1)S(1)} collective-permute-done((bf16[256,128]{1,0:T(8,128)(2,1)S(1)}, bf16[256,128]{1,0:T(8,128)(2,1)S(1)}, u32[]{:S(2)}, u32[]{:S(2)}) %collective-permute-start.16) | collective-permute-done | bytes 65568 | tf_op jit(solution)/shard_map/ppermute | solution.py:48
  45.9 2.0 %collective-permute-start.17 = (bf16[256,128]{1,0:T(8,128)(2,1)S(1)}, bf16[256,128]{1,0:T(8,128)(2,1)S(1)}, u32[]{:S(2)}, u32[]{:S(2)}) collective-permute-start(bf16[256,128]{1,0:T(8,128)(2,1)S(1)} %collective-permute-done.16.sibling_ref), channel_id=1, source_target_pairs={{0,2},{2,4},{3,1},{4,6},{5,3},{6,8},{7,5},{8,10},{9,7},{10,12},{11... | collective-permute-start | bytes 196616 | tf_op jit(solution)/shard_map/ppermute | solution.py:274
  48.0 7.1 %collective-permute-done.17.outer_ref = bf16[256,128]{1,0:T(8,128)(2,1)S(1)} collective-permute-done((bf16[256,128]{1,0:T(8,128)(2,1)S(1)}, bf16[256,128]{1,0:T(8,128)(2,1)S(1)}, u32[]{:S(2)}, u32[]{:S(2)}) %collective-permute-start.17) | collective-permute-done | bytes 65568 | tf_op jit(solution)/shard_map/ppermute | solution.py:274
  55.1 1.0 %refine.1 = bf16[256,128]{1,0:T(8,128)(2,1)} custom-call(bf16[256,128]{1,0:T(8,128)(2,1)S(1)} %collective-permute-done.17.outer_ref, bf16[256,128]{1,0:T(8,128)(2,1)S(1)} %merge.1.here_ref, bf16[256,128]{1,0:T(8,128)(2,1)S(1)} %collective-permute-done.16.sibling_ref, bf16[3,3,128,128]{3,2,1,0:T(8,128)(2,1)S(1)} %copy-done, bf16[1,128]{1,0:T(2,128)(2,1)S(1)} %bitcast.2), custom_call_target="tpu_custom_call" | custom-call | tf_op jit(solution)/shard_map/refine/pallas_call | solution.py:231
  (36 shorter events, 4.2 us)
Async XLA Ops:
  0.0 6.0 %collective-permute-start = (bf16[256,128]{1,0:T(8,128)(2,1)}, bf16[256,128]{1,0:T(8,128)(2,1)S(1)}, u32[]{:S(2)}, u32[]{:S(2)}) collective-permute-start(bf16[256,128]{1,0:T(8,128)(2,1)} %param.7), channel_id=1, source_target_pairs={{0,32},{1,65},{2,34},{3,67},{4,36},{5,69},{6,38},{7,71},{8,40},{9,... | collective-permute-start | bytes 196616 | tf_op jit(solution)/shard_map/ppermute | solution.py:44
  1.4 4.6 %collective-permute-start.1 = (bf16[256,128]{1,0:T(8,128)(2,1)}, bf16[256,128]{1,0:T(8,128)(2,1)S(1)}, u32[]{:S(2)}, u32[]{:S(2)}) collective-permute-start(bf16[256,128]{1,0:T(8,128)(2,1)} %param.7), channel_id=1, source_target_pairs={{0,16},{1,9},{2,18},{3,11},{4,20},{5,13},{6,22},{7,15},{8,24},{9,1... | collective-permute-start | bytes 196616 | tf_op jit(solution)/shard_map/ppermute | solution.py:44
  1.4 5.7 %collective-permute-start.2 = (bf16[256,128]{1,0:T(8,128)(2,1)}, bf16[256,128]{1,0:T(8,128)(2,1)S(1)}, u32[]{:S(2)}, u32[]{:S(2)}) collective-permute-start(bf16[256,128]{1,0:T(8,128)(2,1)} %param.7), channel_id=1, source_target_pairs={{0,48},{1,73},{2,50},{3,75},{4,52},{5,77},{6,54},{7,79},{8,56},{9,... | collective-permute-start | bytes 196616 | tf_op jit(solution)/shard_map/ppermute | solution.py:44
  6.0 2.8 %copy-start.1 = (bf16[256,128]{1,0:T(8,128)(2,1)S(1)}, bf16[256,128]{1,0:T(8,128)(2,1)}, u32[]{:S(2)}) copy-start(bf16[256,128]{1,0:T(8,128)(2,1)} %q_ref.1) | copy-start | bytes 196612
  7.1 16.9 %collective-permute-start.8 = (bf16[1024,128]{1,0:T(8,128)(2,1)S(1)}, bf16[1024,128]{1,0:T(8,128)(2,1)S(1)}, u32[]{:S(2)}, u32[]{:S(2)}) collective-permute-start(bf16[1024,128]{1,0:T(8,128)(2,1)S(1)} %constant_dynamic-update-slice_fusion.refs_4_), channel_id=1, source_target_pairs={{0,1},{1,0},{2,3},{3,2},{4,5},{5,4},{6,7},{7,6},{8,9},{9,8},{10,11... | collective-permute-start | bytes 786440 | tf_op jit(solution)/shard_map/ppermute | solution.py:48
  8.8 6.6 %collective-permute-start.6 = (bf16[256,128]{1,0:T(8,128)(2,1)S(1)}, bf16[256,128]{1,0:T(8,128)(2,1)S(1)}, u32[]{:S(2)}, u32[]{:S(2)}) collective-permute-start(bf16[256,128]{1,0:T(8,128)(2,1)S(1)} %copy-done.1), channel_id=1, source_target_pairs={{0,6},{1,7},{2,4},{3,5},{4,2},{5,3},{6,0},{7,1},{8,14},{9,15},{10,... | collective-permute-start | bytes 196616 | tf_op jit(solution)/shard_map/ppermute | solution.py:44
  11.8 13.9 %collective-permute-start.3 = (bf16[1024,128]{1,0:T(8,128)(2,1)S(1)}, bf16[1024,128]{1,0:T(8,128)(2,1)S(1)}, u32[]{:S(2)}, u32[]{:S(2)}) collective-permute-start(bf16[1024,128]{1,0:T(8,128)(2,1)S(1)} %constant_dynamic-update-slice_fusion.refs_4_), channel_id=1, source_target_pairs={{0,8},{1,17},{2,10},{3,19},{4,12},{5,21},{6,14},{7,23},{8,0},{9,25... | collective-permute-start | bytes 786440 | tf_op jit(solution)/shard_map/ppermute | solution.py:44
  12.2 13.5 %collective-permute-start.4 = (bf16[1024,128]{1,0:T(8,128)(2,1)S(1)}, bf16[1024,128]{1,0:T(8,128)(2,1)S(1)}, u32[]{:S(2)}, u32[]{:S(2)}) collective-permute-start(bf16[1024,128]{1,0:T(8,128)(2,1)S(1)} %constant_dynamic-update-slice_fusion.refs_4_), channel_id=1, source_target_pairs={{0,72},{1,49},{2,74},{3,51},{4,76},{5,53},{6,78},{7,55},{8,64},{9,... | collective-permute-start | bytes 786440 | tf_op jit(solution)/shard_map/ppermute | solution.py:44
  14.7 5.8 %collective-permute-start.7 = (bf16[256,128]{1,0:T(8,128)(2,1)S(1)}, bf16[256,128]{1,0:T(8,128)(2,1)S(1)}, u32[]{:S(2)}, u32[]{:S(2)}) collective-permute-start(bf16[256,128]{1,0:T(8,128)(2,1)S(1)} %copy-done.1), channel_id=1, source_target_pairs={{0,4},{1,5},{2,6},{3,7},{4,0},{5,1},{6,2},{7,3},{8,12},{9,13},{10,... | collective-permute-start | bytes 196616 | tf_op jit(solution)/shard_map/ppermute | solution.py:44
  15.4 7.0 %collective-permute-start.5 = (bf16[256,128]{1,0:T(8,128)(2,1)S(1)}, bf16[256,128]{1,0:T(8,128)(2,1)S(1)}, u32[]{:S(2)}, u32[]{:S(2)}) collective-permute-start(bf16[256,128]{1,0:T(8,128)(2,1)S(1)} %copy-done.1), channel_id=1, source_target_pairs={{0,2},{1,3},{2,0},{3,1},{4,6},{5,7},{6,4},{7,5},{8,10},{9,11},{10,... | collective-permute-start | bytes 196616 | tf_op jit(solution)/shard_map/ppermute | solution.py:44
  20.5 8.2 %collective-permute-start.11 = (bf16[1024,128]{1,0:T(8,128)(2,1)S(1)}, bf16[1024,128]{1,0:T(8,128)(2,1)S(1)}, u32[]{:S(2)}, u32[]{:S(2)}) collective-permute-start(bf16[1024,128]{1,0:T(8,128)(2,1)S(1)} %constant_dynamic-update-slice_fusion.refs_4_), channel_id=1, source_target_pairs={{0,64},{1,33},{2,66},{3,35},{4,68},{5,37},{6,70},{7,39},{8,72},{9,... | collective-permute-start | bytes 786440 | tf_op jit(solution)/shard_map/ppermute | solution.py:44
  25.8 3.2 %collective-permute-start.10 = (bf16[1024,128]{1,0:T(8,128)(2,1)S(1)}, bf16[1024,128]{1,0:T(8,128)(2,1)S(1)}, u32[]{:S(2)}, u32[]{:S(2)}) collective-permute-start(bf16[1024,128]{1,0:T(8,128)(2,1)S(1)} %collective-permute-done.4.refs_4_), channel_id=1, source_target_pairs={{0,1},{1,0},{2,3},{3,2},{4,5},{5,4},{6,7},{7,6},{8,9},{9,8},{10,11... | collective-permute-start | bytes 786440 | tf_op jit(solution)/shard_map/ppermute | solution.py:48
  25.9 3.1 %collective-permute-start.9 = (bf16[1024,128]{1,0:T(8,128)(2,1)S(1)}, bf16[1024,128]{1,0:T(8,128)(2,1)S(1)}, u32[]{:S(2)}, u32[]{:S(2)}) collective-permute-start(bf16[1024,128]{1,0:T(8,128)(2,1)S(1)} %collective-permute-done.3.refs_3_), channel_id=1, source_target_pairs={{0,1},{1,0},{2,3},{3,2},{4,5},{5,4},{6,7},{7,6},{8,9},{9,8},{10,11... | collective-permute-start | bytes 786440 | tf_op jit(solution)/shard_map/ppermute | solution.py:48
  28.7 1.9 %collective-permute-start.12 = (bf16[1024,128]{1,0:T(8,128)(2,1)S(1)}, bf16[1024,128]{1,0:T(8,128)(2,1)S(1)}, u32[]{:S(2)}, u32[]{:S(2)}) collective-permute-start(bf16[1024,128]{1,0:T(8,128)(2,1)S(1)} %collective-permute-done.11.refs_7_.refs_3_.refs_5_), channel_id=1, source_target_pairs={{0,1},{1,0},{2,3},{3,2},{4,5},{5,4},{6,7},{7,6},{8,9},{9,8},{10,11... | collective-permute-start | bytes 786440 | tf_op jit(solution)/shard_map/ppermute | solution.py:48
  31.7 6.3 %collective-permute-start.14 = (bf16[272,128]{1,0:T(8,128)(2,1)S(1)}, bf16[272,128]{1,0:T(8,128)(2,1)S(1)}, u32[]{:S(2)}, u32[]{:S(2)}) collective-permute-start(bf16[272,128]{1,0:T(8,128)(2,1)S(1)} %last_keys.6), channel_id=1, source_target_pairs={{0,6},{1,7},{2,4},{3,5},{4,2},{5,3},{6,0},{7,1},{8,14},{9,15},{10,... | collective-permute-start | bytes 208904 | tf_op jit(solution)/shard_map/ppermute | solution.py:44
  33.3 9.0 %collective-permute-start.13 = (bf16[272,128]{1,0:T(8,128)(2,1)S(1)}, bf16[272,128]{1,0:T(8,128)(2,1)S(1)}, u32[]{:S(2)}, u32[]{:S(2)}) collective-permute-start(bf16[272,128]{1,0:T(8,128)(2,1)S(1)} %last_keys.5), channel_id=1, source_target_pairs={{0,6},{1,7},{2,4},{3,5},{4,2},{5,3},{6,0},{7,1},{8,14},{9,15},{10,... | collective-permute-start | bytes 208904 | tf_op jit(solution)/shard_map/ppermute | solution.py:44
  39.8 4.4 %copy-start.2 = (bf16[128,128]{1,0:T(8,128)(2,1)S(1)}, bf16[128,128]{1,0:T(8,128)(2,1)}, u32[]{:S(2)}) copy-start(bf16[128,128]{1,0:T(8,128)(2,1)} %vw_ref.1) | copy-start | bytes 98308
  39.8 4.4 %copy-start.3 = (bf16[128,128]{1,0:T(8,128)(2,1)S(1)}, bf16[128,128]{1,0:T(8,128)(2,1)}, u32[]{:S(2)}) copy-start(bf16[128,128]{1,0:T(8,128)(2,1)} %ow_ref.1) | copy-start | bytes 98308
  39.8 4.4 %collective-permute-start.15 = (bf16[272,128]{1,0:T(8,128)(2,1)S(1)}, bf16[272,128]{1,0:T(8,128)(2,1)S(1)}, u32[]{:S(2)}, u32[]{:S(2)}) collective-permute-start(bf16[272,128]{1,0:T(8,128)(2,1)S(1)} %last_keys.7), channel_id=1, source_target_pairs={{0,2},{1,3},{2,0},{3,1},{4,6},{5,7},{6,4},{7,5},{8,10},{9,11},{10,... | collective-permute-start | bytes 208904 | tf_op jit(solution)/shard_map/ppermute | solution.py:44
  44.2 10.9 %copy-start = (bf16[3,3,128,128]{3,2,1,0:T(8,128)(2,1)S(1)}, bf16[3,3,128,128]{3,2,1,0:T(8,128)(2,1)}, u32[]{:S(2)}) copy-start(bf16[3,3,128,128]{3,2,1,0:T(8,128)(2,1)} %w_ref.1) | copy-start | bytes 884740
  44.6 10.5 %copy-start.4 = (bf16[128]{0:T(256)(128)(2,1)S(1)}, bf16[128]{0:T(256)(128)(2,1)}, u32[]{:S(2)}) copy-start(bf16[128]{0:T(256)(128)(2,1)} %param.11) | copy-start | bytes 772
  44.6 1.3 %collective-permute-start.16 = (bf16[256,128]{1,0:T(8,128)(2,1)S(1)}, bf16[256,128]{1,0:T(8,128)(2,1)S(1)}, u32[]{:S(2)}, u32[]{:S(2)}) collective-permute-start(bf16[256,128]{1,0:T(8,128)(2,1)S(1)} %merge.1.here_ref), channel_id=1, source_target_pairs={{0,1},{1,0},{2,3},{3,2},{4,5},{5,4},{6,7},{7,6},{8,9},{9,8},{10,11... | collective-permute-start | bytes 196616 | tf_op jit(solution)/shard_map/ppermute | solution.py:48
  45.9 9.2 %collective-permute-start.17 = (bf16[256,128]{1,0:T(8,128)(2,1)S(1)}, bf16[256,128]{1,0:T(8,128)(2,1)S(1)}, u32[]{:S(2)}, u32[]{:S(2)}) collective-permute-start(bf16[256,128]{1,0:T(8,128)(2,1)S(1)} %collective-permute-done.16.sibling_ref), channel_id=1, source_target_pairs={{0,2},{2,4},{3,1},{4,6},{5,3},{6,8},{7,5},{8,10},{9,7},{10,12},{11... | collective-permute-start | bytes 196616 | tf_op jit(solution)/shard_map/ppermute | solution.py:274
where the time goes:
time: 57.1 us; the launch traced here: 56.1 us
  starting transfers between devices  21.1 us (37%)
  waiting for transfers between devices  18.8 us (33%)
  Pallas kernels  15.1 us (26%)
  local copies, waits for them, and re-layouts  0.94 us (2%)
    ppermute x12, starting transfers between devices, trade(): return lax.ppermute(block, AXES, pairs)  16.6 us
    ppermute x12, waiting for transfers between devices, trade(): return lax.ppermute(block, AXES, pairs)  10.4 us
    pallas_call x4, Pallas kernels, keys_call(): pl.pallas_call(functools.partial(keys_kernel, scale, len(queries), len(pi...  7.41 us
    ppermute x1, waiting for transfers between devices, local(): outer = lax.ppermute(sibling, AXES, [p for p in pairs if 0 <= p[1] < 128])  7.12 us
    pallas_call x4, Pallas kernels, last_call(): pl.pallas_call(functools.partial(last_kernel, scale, row, len(pieces), pa...  6.27 us
    ppermute x5, starting transfers between devices, swap(): return lax.ppermute(block, AXES, [(i, i ^ 1) for i in range(128)])  2.53 us
    ppermute x1, starting transfers between devices, local(): outer = lax.ppermute(sibling, AXES, [p for p in pairs if 0 <= p[1] < 128])  2.03 us
    ppermute x5, waiting for transfers between devices, swap(): return lax.ppermute(block, AXES, [(i, i ^ 1) for i in range(128)])  1.25 us
  transfers between devices with their start and end apart: 18, of which 7 were waited for; matrix products, arithmetic and copies ran while one was open for 2% of the time, Pallas kernels for 22%

commit v1 on v0

--- a/solution.py
+++ b/solution.py
@@ -153,8 +153,7 @@
     refs = list(refs)
     q_ref, peak_ref, sum_ref = refs[:3]
     pieces, refs = refs[3 : 3 + nk], refs[3 + nk :]
-    outs = refs[-1:] if packed else refs[-2:]
-    arrived = refs[: len(refs) - len(outs)]
+    outs = refs
     queries = blocks_of([q_ref])
     state = [
         (peak_ref[row + at : row + at + ROWS], sum_ref[row + at : row + at + ROWS])
@@ -163,8 +162,6 @@
     state = attend(queries, pieces, state, scale)
     level = jnp.concatenate([peak for peak, _ in state], axis=0) * scale
     weighted = jnp.concatenate([total for _, total in state], axis=0)
-    for part in arrived:
-        level, weighted = absorb(level, weighted, part)
     if packed:
         pack(level, weighted, outs[0])
     else:
@@ -172,7 +169,7 @@
         outs[1][...] = weighted
 
 
-def last_call(query, row, state, pieces, scale, arrived=(), packed=True):
+def last_call(query, row, state, pieces, scale, packed=True):
     shapes = jax.ShapeDtypeStruct((272, 128), jnp.bfloat16)
     if not packed:
         shapes = [
@@ -182,12 +179,12 @@
     return pl.pallas_call(
         functools.partial(last_kernel, scale, row, len(pieces), packed),
         out_shape=shapes,
-        in_specs=[VMEM] * (3 + len(pieces) + len(arrived)),
+        in_specs=[VMEM] * (3 + len(pieces)),
         out_specs=VMEM if packed else [VMEM] * 2,
         compiler_params=params(),
         cost_estimate=cost(256, sum(p.shape[0] for p in pieces)),
         name="last_keys",
-    )(query, *state, *pieces, *arrived)
+    )(query, *state, *pieces)
 
 
 def merge_kernel(q_ref, vw_ref, ow_ref, level_ref, sum_ref, *refs):
@@ -214,12 +211,19 @@
     )(query, vw, ow, *own, *parts)
 
 
-def conv_kernel(outer_ref, here_ref, sibling_ref, w_ref, bias_ref, out_ref):
+def taps_of(row_ref, w_ref, a):
+    taps = jnp.concatenate([w_ref[a, b] for b in range(3)], axis=1)
+    return jnp.dot(row_ref[...], taps, preferred_element_type=jnp.float32)
+
+
+def near_rows_kernel(here_ref, sibling_ref, w_ref, out_ref):
     odd = lax.axis_index("ka") % 2
-    total = jnp.zeros((256, 384), jnp.float32)
-    for row, a in ((outer_ref, 2 * odd), (here_ref, 1), (sibling_ref, 2 - 2 * odd)):
-        taps = jnp.concatenate([w_ref[a, b] for b in range(3)], axis=1)
-        total = total + jnp.dot(row[...], taps, preferred_element_type=jnp.float32)
+    out_ref[...] = taps_of(here_ref, w_ref, 1) + taps_of(sibling_ref, w_ref, 2 - 2 * odd)
+
+
+def refine_kernel(outer_ref, here_ref, near_ref, w_ref, bias_ref, out_ref):
+    odd = lax.axis_index("ka") % 2
+    total = near_ref[...] + taps_of(outer_ref, w_ref, 2 * odd)
     at = lax.broadcasted_iota(jnp.int32, (256, 128), 0)
     left = jnp.where(at == 0, 0.0, pltpu.roll(total[:, 0:128], 1, 0))
     right = jnp.where(at == 255, 0.0, pltpu.roll(total[:, 256:384], 255, 0))
@@ -227,15 +231,26 @@
     out_ref[...] = (here_ref[...].astype(jnp.float32) + jax.nn.gelu(conv)).astype(jnp.bfloat16)
 
 
-def conv_call(outer, here, sibling, w, bias):
-    return pl.pallas_call(
-        conv_kernel,
+def near_rows_call(here, sibling, w):
+    return pl.pallas_call(
+        near_rows_kernel,
+        out_shape=jax.ShapeDtypeStruct((256, 384), jnp.float32),
+        in_specs=[VMEM] * 3,
+        out_specs=VMEM,
+        compiler_params=params(),
+        name="near_rows",
+    )(here, sibling, w)
+
+
+def refine_call(outer, here, near, w, bias):
+    return pl.pallas_call(
+        refine_kernel,
         out_shape=jax.ShapeDtypeStruct((256, 128), jnp.bfloat16),
         in_specs=[VMEM] * 5,
         out_specs=VMEM,
         compiler_params=params(),
         name="refine",
-    )(outer, here, sibling, w, bias.reshape(1, 128))
+    )(outer, here, near, w, bias.reshape(1, 128))
 
 
 def local(feat_first, feat_second, value_weight, out_weight, conv_weight, conv_bias):
@@ -244,7 +259,7 @@
     near = [trade(feat_second, kind, "x", "z") for kind in ("AB", "A", "B")]
     queries = [trade(feat_first, kind, "y") for kind in ("AB", "A", "B")]
     mine = jnp.concatenate([feat_second] + near, axis=0)
-    far_ab, far_a, far_b = [trade(mine, kind, "z", "x") for kind in ("AB", "A", "B")]
+    far_a, far_b, far_ab = [trade(mine, kind, "z", "x") for kind in ("A", "B", "AB")]
     twin = swap(mine)
     query_ab, query_a, query_b = queries
     queries = [feat_first, query_a, query_b, query_ab]
@@ -259,20 +274,21 @@
     away = keys_call(queries[2:], [twin_a, twin_b], scale, other, 256)
     twin_ab, away = fence((twin_ab, away))
     tail = [far_ab, twin_ab]
-    across = last_call(query_ab, 256, away, tail, scale)
-    across = trade(across, "B", "y")
+    from_ab = last_call(query_ab, 256, away, tail, scale)
+    from_ab = trade(from_ab, "AB", "y")
     from_b = last_call(query_b, 0, away, tail, scale)
     from_b = trade(from_b, "B", "y")
-    from_a = last_call(query_a, 0, other, [twin_a, twin_b] + tail, scale, (across,))
+    from_a = last_call(query_a, 0, other, [twin_a, twin_b] + tail, scale)
     from_a = trade(from_a, "A", "y")
     own = last_call(
         feat_first, 0, state, [far_a, far_b, twin_a, twin_b] + tail, scale, packed=False
     )
-    mixed = merge_call(feat_first, value_weight, out_weight, own, (from_b, from_a))
+    mixed = merge_call(feat_first, value_weight, out_weight, own, (from_ab, from_b, from_a))
     sibling = swap(mixed)
     pairs = [(i, i - 2 if i % 2 else i + 2) for i in range(128)]
     outer = lax.ppermute(sibling, AXES, [p for p in pairs if 0 <= p[1] < 128])
-    refined = conv_call(outer, mixed, sibling, conv_weight, conv_bias)
+    rows = near_rows_call(mixed, sibling, conv_weight)
+    refined = refine_call(outer, mixed, rows, conv_weight, conv_bias)
     return refined.reshape(1, 256, 128)
 
 

time: 57.1 us -> 55.2 us (0.967)
  the two profiles are of different devices: /device:TPU:6 before, /device:TPU:64 now
where the time goes in v1:
time: 55.2 us; the launch traced here: 55.1 us
  starting transfers between devices  20.3 us (37%)
  waiting for transfers between devices  18.3 us (33%)
  Pallas kernels  15.4 us (28%)
  local copies, waits for them, and re-layouts  0.94 us (2%)
    ppermute x12, starting transfers between devices, trade(): return lax.ppermute(block, AXES, pairs)  16.5 us
    ppermute x12, waiting for transfers between devices, trade(): return lax.ppermute(block, AXES, pairs)  9.78 us
    pallas_call x4, Pallas kernels, keys_call(): pl.pallas_call(functools.partial(keys_kernel, scale, len(queries), len(pi...  7.44 us
    ppermute x1, waiting for transfers between devices, local(): outer = lax.ppermute(sibling, AXES, [p for p in pairs if 0 <= p[1] < 128])  7.22 us
    pallas_call x4, Pallas kernels, last_call(): pl.pallas_call(functools.partial(last_kernel, scale, row, len(pieces), pa...  6.3 us
    ppermute x1, starting transfers between devices, local(): outer = lax.ppermute(sibling, AXES, [p for p in pairs if 0 <= p[1] < 128])  2.84 us
    ppermute x5, waiting for transfers between devices, swap(): return lax.ppermute(block, AXES, [(i, i ^ 1) for i in range(128)])  1.25 us
  transfers between devices with their start and end apart: 18, of which 8 were waited for; matrix products, arithmetic and copies ran while one was open for 2% of the time, Pallas kernels for 22%

profile of v1, /device:TPU:64, one launch (start us, length us, event | category | flops | bytes accessed | tf_op | source)
XLA Modules:
  0.0 55.1 jit_solution(17177744286441874284)
XLA Ops:
  0.0 3.0 %collective-permute-start = (bf16[256,128]{1,0:T(8,128)(2,1)}, bf16[256,128]{1,0:T(8,128)(2,1)S(1)}, u32[]{:S(2)}, u32[]{:S(2)}) collective-permute-start(bf16[256,128]{1,0:T(8,128)(2,1)} %param.7), channel_id=1, source_target_pairs={{0,32},{1,65},{2,34},{3,67},{4,36},{5,69},{6,38},{7,71},{8,40},{9,... | collective-permute-start | bytes 196616 | tf_op jit(solution)/shard_map/ppermute | solution.py:44
  4.2 0.9 %constant_dynamic-update-slice_fusion.3 = bf16[1024,128]{1,0:T(8,128)(2,1)S(1)} fusion(bf16[256,128]{1,0:T(8,128)(2,1)} %param.7), kind=kLoop, calls=%fused_computation.3 | loop fusion | bytes 131072
  5.0 0.9 %collective-permute-done = bf16[256,128]{1,0:T(8,128)(2,1)S(1)} collective-permute-done((bf16[256,128]{1,0:T(8,128)(2,1)}, bf16[256,128]{1,0:T(8,128)(2,1)S(1)}, u32[]{:S(2)}, u32[]{:S(2)}) %collective-permute-start) | collective-permute-done | bytes 65568 | tf_op jit(solution)/shard_map/ppermute | solution.py:44
  6.0 1.5 %collective-permute-done.1 = bf16[256,128]{1,0:T(8,128)(2,1)S(1)} collective-permute-done((bf16[256,128]{1,0:T(8,128)(2,1)}, bf16[256,128]{1,0:T(8,128)(2,1)S(1)}, u32[]{:S(2)}, u32[]{:S(2)}) %collective-permute-start.1) | collective-permute-done | bytes 65568 | tf_op jit(solution)/shard_map/ppermute | solution.py:44
  7.5 1.8 %collective-permute-done.2 = bf16[256,128]{1,0:T(8,128)(2,1)S(1)} collective-permute-done((bf16[256,128]{1,0:T(8,128)(2,1)}, bf16[256,128]{1,0:T(8,128)(2,1)S(1)}, u32[]{:S(2)}, u32[]{:S(2)}) %collective-permute-start.2) | collective-permute-done | bytes 65568 | tf_op jit(solution)/shard_map/ppermute | solution.py:44
  9.4 3.1 %collective-permute-start.6 = (bf16[256,128]{1,0:T(8,128)(2,1)S(1)}, bf16[256,128]{1,0:T(8,128)(2,1)S(1)}, u32[]{:S(2)}, u32[]{:S(2)}) collective-permute-start(bf16[256,128]{1,0:T(8,128)(2,1)S(1)} %copy-done.1), channel_id=1, source_target_pairs={{0,6},{1,7},{2,4},{3,5},{4,2},{5,3},{6,0},{7,1},{8,14},{9,15},{10,... | collective-permute-start | bytes 196616 | tf_op jit(solution)/shard_map/ppermute | solution.py:44
  12.5 1.6 %collective-permute-start.3 = (bf16[1024,128]{1,0:T(8,128)(2,1)S(1)}, bf16[1024,128]{1,0:T(8,128)(2,1)S(1)}, u32[]{:S(2)}, u32[]{:S(2)}) collective-permute-start(bf16[1024,128]{1,0:T(8,128)(2,1)S(1)} %constant_dynamic-update-slice_fusion.refs_4_), channel_id=1, source_target_pairs={{0,8},{1,17},{2,10},{3,19},{4,12},{5,21},{6,14},{7,23},{8,0},{9,25... | collective-permute-start | bytes 786440 | tf_op jit(solution)/shard_map/ppermute | solution.py:44
  14.1 0.6 %collective-permute-start.7 = (bf16[256,128]{1,0:T(8,128)(2,1)S(1)}, bf16[256,128]{1,0:T(8,128)(2,1)S(1)}, u32[]{:S(2)}, u32[]{:S(2)}) collective-permute-start(bf16[256,128]{1,0:T(8,128)(2,1)S(1)} %copy-done.1), channel_id=1, source_target_pairs={{0,4},{1,5},{2,6},{3,7},{4,0},{5,1},{6,2},{7,3},{8,12},{9,13},{10,... | collective-permute-start | bytes 196616 | tf_op jit(solution)/shard_map/ppermute | solution.py:44
  15.5 4.6 %collective-permute-done.7.refs_3_.refs_2_.refs_1_.refs_0_ = bf16[256,128]{1,0:T(8,128)(2,1)S(1)} collective-permute-done((bf16[256,128]{1,0:T(8,128)(2,1)S(1)}, bf16[256,128]{1,0:T(8,128)(2,1)S(1)}, u32[]{:S(2)}, u32[]{:S(2)}) %collective-permute-start.7) | collective-permute-done | bytes 65568 | tf_op jit(solution)/shard_map/ppermute | solution.py:44
  20.1 2.3 %collective-permute-start.11 = (bf16[1024,128]{1,0:T(8,128)(2,1)S(1)}, bf16[1024,128]{1,0:T(8,128)(2,1)S(1)}, u32[]{:S(2)}, u32[]{:S(2)}) collective-permute-start(bf16[1024,128]{1,0:T(8,128)(2,1)S(1)} %constant_dynamic-update-slice_fusion.refs_4_), channel_id=1, source_target_pairs={{0,64},{1,33},{2,66},{3,35},{4,68},{5,37},{6,70},{7,39},{8,72},{9,... | collective-permute-start | bytes 786440 | tf_op jit(solution)/shard_map/ppermute | solution.py:44
  22.4 1.6 %keys.4 = (f32[1024,128]{1,0:T(8,128)S(1)}, f32[1024,256]{1,0:T(8,128)S(1)}) custom-call(bf16[256,128]{1,0:T(8,128)(2,1)S(1)} %copy-done.1, bf16[256,128]{1,0:T(8,128)(2,1)S(1)} %collective-permute-done.5.refs_1_.refs_0_, bf16[256,128]{1,0:T(8,128)(2,1)S(1)} %collective-permute-done.6.refs_2_.refs_1_.refs_0_, ...), custom_call_target="tpu_custom_call" | custom-call | flops 805306368 | bytes 1048576 | tf_op jit(solution)/shard_map/keys/pallas_call | solution.py:103
  24.0 1.7 %keys.5 = (f32[1024,128]{1,0:T(8,128)S(1)}, f32[1024,256]{1,0:T(8,128)S(1)}) custom-call(bf16[256,128]{1,0:T(8,128)(2,1)S(1)} %copy-done.1, bf16[256,128]{1,0:T(8,128)(2,1)S(1)} %collective-permute-done.5.refs_1_.refs_0_, bf16[256,128]{1,0:T(8,128)(2,1)S(1)} %collective-permute-done.6.refs_2_.refs_1_.refs_0_, ...), custom_call_target="tpu_custom_call" | custom-call | flops 805306368 | bytes 1048576 | tf_op jit(solution)/shard_map/keys/pallas_call | solution.py:103
  26.3 2.4 %keys.6 = (f32[768,128]{1,0:T(8,128)S(1)}, f32[768,256]{1,0:T(8,128)S(1)}) custom-call(bf16[256,128]{1,0:T(8,128)(2,1)S(1)} %collective-permute-done.5.refs_1_.refs_0_, bf16[256,128]{1,0:T(8,128)(2,1)S(1)} %collective-permute-done.6.refs_2_.refs_1_.refs_0_, bf16[256,128]{1,0:T(8,128)(2,1)S(1)} %collective-permute-done.7.refs_3_.refs_2_.refs_1_.refs_0_, ...), custom_call_target="tpu_custom_call" | custom-call | flops 1207959552 | bytes 1048576 | tf_op jit(solution)/shard_map/keys/pallas_call | solution.py:103
  28.9 1.7 %keys.7 = (f32[512,128]{1,0:T(8,128)S(1)}, f32[512,256]{1,0:T(8,128)S(1)}) custom-call(bf16[256,128]{1,0:T(8,128)(2,1)S(1)} %collective-permute-done.6.refs_2_.refs_1_.refs_0_, bf16[256,128]{1,0:T(8,128)(2,1)S(1)} %collective-permute-done.7.refs_3_.refs_2_.refs_1_.refs_0_, bf16[1024,128]{1,0:T(8,128)(2,1)S(1)} %collective-permute-done.9.refs_2_.refs_5_.refs_3_, ...), custom_call_target="tpu_custom_call" | custom-call | flops 805306368 | bytes 1048576 | tf_op jit(solution)/shard_map/keys/pallas_call | solution.py:103
  30.7 1.8 %last_keys.7 = bf16[272,128]{1,0:T(8,128)(2,1)S(1)} custom-call(bf16[256,128]{1,0:T(8,128)(2,1)S(1)} %collective-permute-done.5.refs_1_.refs_0_, f32[768,128]{1,0:T(8,128)S(1)} %get-tuple-element.42.refs_4_.refs_1_, f32[768,256]{1,0:T(8,128)S(1)} %get-tuple-element.43.refs_5_.refs_2_, bf16[1024,128]{1,0:T(8,128)(2,1)S(1)} %collective-permute-done.9.refs_2_.refs_5_.refs_3_, ...), custom_call_target="tpu_custom_call" | custom-call | flops 805306368 | bytes 1048576 | tf_op jit(solution)/shard_map/last_keys/pallas_call | solution.py:179
  32.8 1.1 %last_keys.6 = bf16[272,128]{1,0:T(8,128)(2,1)S(1)} custom-call(bf16[256,128]{1,0:T(8,128)(2,1)S(1)} %collective-permute-done.6.refs_2_.refs_1_.refs_0_, f32[512,128]{1,0:T(8,128)S(1)} %get-tuple-element.49.refs_1_, f32[512,256]{1,0:T(8,128)S(1)} %get-tuple-element.50.refs_2_, bf16[1024,128]{1,0:T(8,128)(2,1)S(1)} %collective-permute-done.11.refs_7_.refs_3_.refs_5_, ...), custom_call_target="tpu_custom_call" | custom-call | flops 402653184 | bytes 1048576 | tf_op jit(solution)/shard_map/last_keys/pallas_call | solution.py:179
  33.9 1.1 %collective-permute-start.14 = (bf16[272,128]{1,0:T(8,128)(2,1)S(1)}, bf16[272,128]{1,0:T(8,128)(2,1)S(1)}, u32[]{:S(2)}, u32[]{:S(2)}) collective-permute-start(bf16[272,128]{1,0:T(8,128)(2,1)S(1)} %last_keys.6), channel_id=1, source_target_pairs={{0,6},{1,7},{2,4},{3,5},{4,2},{5,3},{6,0},{7,1},{8,14},{9,15},{10,... | collective-permute-start | bytes 208904 | tf_op jit(solution)/shard_map/ppermute | solution.py:44
  35.0 1.1 %last_keys.5 = bf16[272,128]{1,0:T(8,128)(2,1)S(1)} custom-call(bf16[256,128]{1,0:T(8,128)(2,1)S(1)} %collective-permute-done.7.refs_3_.refs_2_.refs_1_.refs_0_, f32[512,128]{1,0:T(8,128)S(1)} %get-tuple-element.49.refs_1_, f32[512,256]{1,0:T(8,128)S(1)} %get-tuple-element.50.refs_2_, bf16[1024,128]{1,0:T(8,128)(2,1)S(1)} %collective-permute-done.11.refs_7_.refs_3_.refs_5_, ...), custom_call_target="tpu_custom_call" | custom-call | flops 402653184 | bytes 1048576 | tf_op jit(solution)/shard_map/last_keys/pallas_call | solution.py:179
  36.1 3.0 %collective-permute-start.13 = (bf16[272,128]{1,0:T(8,128)(2,1)S(1)}, bf16[272,128]{1,0:T(8,128)(2,1)S(1)}, u32[]{:S(2)}, u32[]{:S(2)}) collective-permute-start(bf16[272,128]{1,0:T(8,128)(2,1)S(1)} %last_keys.5), channel_id=1, source_target_pairs={{0,4},{1,5},{2,6},{3,7},{4,0},{5,1},{6,2},{7,3},{8,12},{9,13},{10,... | collective-permute-start | bytes 208904 | tf_op jit(solution)/shard_map/ppermute | solution.py:44
  39.1 2.4 %last_keys.4 = (f32[256,128]{1,0:T(8,128)S(1)}, f32[256,256]{1,0:T(8,128)S(1)}) custom-call(bf16[256,128]{1,0:T(8,128)(2,1)S(1)} %copy-done.1, f32[1024,128]{1,0:T(8,128)S(1)} %get-tuple-element.35.refs_5_.refs_1_, f32[1024,256]{1,0:T(8,128)S(1)} %get-tuple-element.36.refs_6_.refs_2_, bf16[1024,128]{1,0:T(8,128)(2,1)S(1)} %collective-permute-done.3.refs_3_, ...), custom_call_target="tpu_custom_call" | custom-call | flops 1207959552 | bytes 1048576 | tf_op jit(solution)/shard_map/last_keys/pallas_call | solution.py:179
  42.5 1.2 %collective-permute-done.16.sibling_ref = bf16[256,128]{1,0:T(8,128)(2,1)S(1)} collective-permute-done((bf16[256,128]{1,0:T(8,128)(2,1)S(1)}, bf16[256,128]{1,0:T(8,128)(2,1)S(1)}, u32[]{:S(2)}, u32[]{:S(2)}) %collective-permute-start.16) | collective-permute-done | bytes 65568 | tf_op jit(solution)/shard_map/ppermute | solution.py:48
  43.8 2.8 %collective-permute-start.17 = (bf16[256,128]{1,0:T(8,128)(2,1)S(1)}, bf16[256,128]{1,0:T(8,128)(2,1)S(1)}, u32[]{:S(2)}, u32[]{:S(2)}) collective-permute-start(bf16[256,128]{1,0:T(8,128)(2,1)S(1)} %collective-permute-done.16.sibling_ref), channel_id=1, source_target_pairs={{0,2},{2,4},{3,1},{4,6},{5,3},{6,8},{7,5},{8,10},{9,7},{10,12},{11... | collective-permute-start | bytes 196616 | tf_op jit(solution)/shard_map/ppermute | solution.py:289
  46.9 7.2 %collective-permute-done.17.outer_ref = bf16[256,128]{1,0:T(8,128)(2,1)S(1)} collective-permute-done((bf16[256,128]{1,0:T(8,128)(2,1)S(1)}, bf16[256,128]{1,0:T(8,128)(2,1)S(1)}, u32[]{:S(2)}, u32[]{:S(2)}) %collective-permute-start.17) | collective-permute-done | bytes 65568 | tf_op jit(solution)/shard_map/ppermute | solution.py:289
  54.2 0.9 %refine.1 = bf16[256,128]{1,0:T(8,128)(2,1)} custom-call(bf16[256,128]{1,0:T(8,128)(2,1)S(1)} %collective-permute-done.17.outer_ref, bf16[256,128]{1,0:T(8,128)(2,1)S(1)} %merge.1.here_ref, f32[256,384]{1,0:T(8,128)S(1)} %near_rows.1.near_ref, bf16[3,3,128,128]{3,2,1,0:T(8,128)(2,1)S(1)} %copy-done, bf16[1,128]{1,0:T(2,128)(2,1)S(1)} %bitcast.2), custom_call_target="tpu_custom_call" | custom-call | tf_op jit(solution)/shard_map/refine/pallas_call | solution.py:246
  (37 shorter events, 4.5 us)
Async XLA Ops:
  0.0 6.0 %collective-permute-start = (bf16[256,128]{1,0:T(8,128)(2,1)}, bf16[256,128]{1,0:T(8,128)(2,1)S(1)}, u32[]{:S(2)}, u32[]{:S(2)}) collective-permute-start(bf16[256,128]{1,0:T(8,128)(2,1)} %param.7), channel_id=1, source_target_pairs={{0,32},{1,65},{2,34},{3,67},{4,36},{5,69},{6,38},{7,71},{8,40},{9,... | collective-permute-start | bytes 196616 | tf_op jit(solution)/shard_map/ppermute | solution.py:44
  3.0 4.5 %collective-permute-start.1 = (bf16[256,128]{1,0:T(8,128)(2,1)}, bf16[256,128]{1,0:T(8,128)(2,1)S(1)}, u32[]{:S(2)}, u32[]{:S(2)}) collective-permute-start(bf16[256,128]{1,0:T(8,128)(2,1)} %param.7), channel_id=1, source_target_pairs={{0,16},{1,9},{2,18},{3,11},{4,20},{5,13},{6,22},{7,15},{8,24},{9,1... | collective-permute-start | bytes 196616 | tf_op jit(solution)/shard_map/ppermute | solution.py:44
  3.6 5.7 %collective-permute-start.2 = (bf16[256,128]{1,0:T(8,128)(2,1)}, bf16[256,128]{1,0:T(8,128)(2,1)S(1)}, u32[]{:S(2)}, u32[]{:S(2)}) collective-permute-start(bf16[256,128]{1,0:T(8,128)(2,1)} %param.7), channel_id=1, source_target_pairs={{0,48},{1,73},{2,50},{3,75},{4,52},{5,77},{6,54},{7,79},{8,56},{9,... | collective-permute-start | bytes 196616 | tf_op jit(solution)/shard_map/ppermute | solution.py:44
  7.5 1.9 %copy-start.1 = (bf16[256,128]{1,0:T(8,128)(2,1)S(1)}, bf16[256,128]{1,0:T(8,128)(2,1)}, u32[]{:S(2)}) copy-start(bf16[256,128]{1,0:T(8,128)(2,1)} %q_ref.1) | copy-start | bytes 196612
  9.3 14.7 %collective-permute-start.8 = (bf16[1024,128]{1,0:T(8,128)(2,1)S(1)}, bf16[1024,128]{1,0:T(8,128)(2,1)S(1)}, u32[]{:S(2)}, u32[]{:S(2)}) collective-permute-start(bf16[1024,128]{1,0:T(8,128)(2,1)S(1)} %constant_dynamic-update-slice_fusion.refs_4_), channel_id=1, source_target_pairs={{0,1},{1,0},{2,3},{3,2},{4,5},{5,4},{6,7},{7,6},{8,9},{9,8},{10,11... | collective-permute-start | bytes 786440 | tf_op jit(solution)/shard_map/ppermute | solution.py:48
  9.4 5.8 %collective-permute-start.6 = (bf16[256,128]{1,0:T(8,128)(2,1)S(1)}, bf16[256,128]{1,0:T(8,128)(2,1)S(1)}, u32[]{:S(2)}, u32[]{:S(2)}) collective-permute-start(bf16[256,128]{1,0:T(8,128)(2,1)S(1)} %copy-done.1), channel_id=1, source_target_pairs={{0,6},{1,7},{2,4},{3,5},{4,2},{5,3},{6,0},{7,1},{8,14},{9,15},{10,... | collective-permute-start | bytes 196616 | tf_op jit(solution)/shard_map/ppermute | solution.py:44
  12.5 13.2 %collective-permute-start.3 = (bf16[1024,128]{1,0:T(8,128)(2,1)S(1)}, bf16[1024,128]{1,0:T(8,128)(2,1)S(1)}, u32[]{:S(2)}, u32[]{:S(2)}) collective-permute-start(bf16[1024,128]{1,0:T(8,128)(2,1)S(1)} %constant_dynamic-update-slice_fusion.refs_4_), channel_id=1, source_target_pairs={{0,8},{1,17},{2,10},{3,19},{4,12},{5,21},{6,14},{7,23},{8,0},{9,25... | collective-permute-start | bytes 786440 | tf_op jit(solution)/shard_map/ppermute | solution.py:44
  14.1 11.6 %collective-permute-start.4 = (bf16[1024,128]{1,0:T(8,128)(2,1)S(1)}, bf16[1024,128]{1,0:T(8,128)(2,1)S(1)}, u32[]{:S(2)}, u32[]{:S(2)}) collective-permute-start(bf16[1024,128]{1,0:T(8,128)(2,1)S(1)} %constant_dynamic-update-slice_fusion.refs_4_), channel_id=1, source_target_pairs={{0,72},{1,49},{2,74},{3,51},{4,76},{5,53},{6,78},{7,55},{8,64},{9,... | collective-permute-start | bytes 786440 | tf_op jit(solution)/shard_map/ppermute | solution.py:44
  14.1 6.0 %collective-permute-start.7 = (bf16[256,128]{1,0:T(8,128)(2,1)S(1)}, bf16[256,128]{1,0:T(8,128)(2,1)S(1)}, u32[]{:S(2)}, u32[]{:S(2)}) collective-permute-start(bf16[256,128]{1,0:T(8,128)(2,1)S(1)} %copy-done.1), channel_id=1, source_target_pairs={{0,4},{1,5},{2,6},{3,7},{4,0},{5,1},{6,2},{7,3},{8,12},{9,13},{10,... | collective-permute-start | bytes 196616 | tf_op jit(solution)/shard_map/ppermute | solution.py:44
  15.2 7.2 %collective-permute-start.5 = (bf16[256,128]{1,0:T(8,128)(2,1)S(1)}, bf16[256,128]{1,0:T(8,128)(2,1)S(1)}, u32[]{:S(2)}, u32[]{:S(2)}) collective-permute-start(bf16[256,128]{1,0:T(8,128)(2,1)S(1)} %copy-done.1), channel_id=1, source_target_pairs={{0,2},{1,3},{2,0},{3,1},{4,6},{5,7},{6,4},{7,5},{8,10},{9,11},{10,... | collective-permute-start | bytes 196616 | tf_op jit(solution)/shard_map/ppermute | solution.py:44
  20.1 8.6 %collective-permute-start.11 = (bf16[1024,128]{1,0:T(8,128)(2,1)S(1)}, bf16[1024,128]{1,0:T(8,128)(2,1)S(1)}, u32[]{:S(2)}, u32[]{:S(2)}) collective-permute-start(bf16[1024,128]{1,0:T(8,128)(2,1)S(1)} %constant_dynamic-update-slice_fusion.refs_4_), channel_id=1, source_target_pairs={{0,64},{1,33},{2,66},{3,35},{4,68},{5,37},{6,70},{7,39},{8,72},{9,... | collective-permute-start | bytes 786440 | tf_op jit(solution)/shard_map/ppermute | solution.py:44
  25.8 3.2 %collective-permute-start.10 = (bf16[1024,128]{1,0:T(8,128)(2,1)S(1)}, bf16[1024,128]{1,0:T(8,128)(2,1)S(1)}, u32[]{:S(2)}, u32[]{:S(2)}) collective-permute-start(bf16[1024,128]{1,0:T(8,128)(2,1)S(1)} %collective-permute-done.4.refs_4_), channel_id=1, source_target_pairs={{0,1},{1,0},{2,3},{3,2},{4,5},{5,4},{6,7},{7,6},{8,9},{9,8},{10,11... | collective-permute-start | bytes 786440 | tf_op jit(solution)/shard_map/ppermute | solution.py:48
  25.8 3.1 %collective-permute-start.9 = (bf16[1024,128]{1,0:T(8,128)(2,1)S(1)}, bf16[1024,128]{1,0:T(8,128)(2,1)S(1)}, u32[]{:S(2)}, u32[]{:S(2)}) collective-permute-start(bf16[1024,128]{1,0:T(8,128)(2,1)S(1)} %collective-permute-done.3.refs_3_), channel_id=1, source_target_pairs={{0,1},{1,0},{2,3},{3,2},{4,5},{5,4},{6,7},{7,6},{8,9},{9,8},{10,11... | collective-permute-start | bytes 786440 | tf_op jit(solution)/shard_map/ppermute | solution.py:48
  28.7 1.9 %collective-permute-start.12 = (bf16[1024,128]{1,0:T(8,128)(2,1)S(1)}, bf16[1024,128]{1,0:T(8,128)(2,1)S(1)}, u32[]{:S(2)}, u32[]{:S(2)}) collective-permute-start(bf16[1024,128]{1,0:T(8,128)(2,1)S(1)} %collective-permute-done.11.refs_7_.refs_3_.refs_5_), channel_id=1, source_target_pairs={{0,1},{1,0},{2,3},{3,2},{4,5},{5,4},{6,7},{7,6},{8,9},{9,8},{10,11... | collective-permute-start | bytes 786440 | tf_op jit(solution)/shard_map/ppermute | solution.py:48
  32.4 9.0 %collective-permute-start.15 = (bf16[272,128]{1,0:T(8,128)(2,1)S(1)}, bf16[272,128]{1,0:T(8,128)(2,1)S(1)}, u32[]{:S(2)}, u32[]{:S(2)}) collective-permute-start(bf16[272,128]{1,0:T(8,128)(2,1)S(1)} %last_keys.7), channel_id=1, source_target_pairs={{0,2},{1,3},{2,0},{3,1},{4,6},{5,7},{6,4},{7,5},{8,10},{9,11},{10,... | collective-permute-start | bytes 208904 | tf_op jit(solution)/shard_map/ppermute | solution.py:44
  33.9 7.6 %collective-permute-start.14 = (bf16[272,128]{1,0:T(8,128)(2,1)S(1)}, bf16[272,128]{1,0:T(8,128)(2,1)S(1)}, u32[]{:S(2)}, u32[]{:S(2)}) collective-permute-start(bf16[272,128]{1,0:T(8,128)(2,1)S(1)} %last_keys.6), channel_id=1, source_target_pairs={{0,6},{1,7},{2,4},{3,5},{4,2},{5,3},{6,0},{7,1},{8,14},{9,15},{10,... | collective-permute-start | bytes 208904 | tf_op jit(solution)/shard_map/ppermute | solution.py:44
  36.1 5.9 %copy-start.2 = (bf16[128,128]{1,0:T(8,128)(2,1)S(1)}, bf16[128,128]{1,0:T(8,128)(2,1)}, u32[]{:S(2)}) copy-start(bf16[128,128]{1,0:T(8,128)(2,1)} %vw_ref.1) | copy-start | bytes 98308
  36.1 5.9 %copy-start.3 = (bf16[128,128]{1,0:T(8,128)(2,1)S(1)}, bf16[128,128]{1,0:T(8,128)(2,1)}, u32[]{:S(2)}) copy-start(bf16[128,128]{1,0:T(8,128)(2,1)} %ow_ref.1) | copy-start | bytes 98308
  36.1 5.9 %collective-permute-start.13 = (bf16[272,128]{1,0:T(8,128)(2,1)S(1)}, bf16[272,128]{1,0:T(8,128)(2,1)S(1)}, u32[]{:S(2)}, u32[]{:S(2)}) collective-permute-start(bf16[272,128]{1,0:T(8,128)(2,1)S(1)} %last_keys.5), channel_id=1, source_target_pairs={{0,4},{1,5},{2,6},{3,7},{4,0},{5,1},{6,2},{7,3},{8,12},{9,13},{10,... | collective-permute-start | bytes 208904 | tf_op jit(solution)/shard_map/ppermute | solution.py:44
  42.0 4.7 %copy-start = (bf16[3,3,128,128]{3,2,1,0:T(8,128)(2,1)S(1)}, bf16[3,3,128,128]{3,2,1,0:T(8,128)(2,1)}, u32[]{:S(2)}) copy-start(bf16[3,3,128,128]{3,2,1,0:T(8,128)(2,1)} %w_ref.3) | copy-start | bytes 884740
  42.5 1.3 %collective-permute-start.16 = (bf16[256,128]{1,0:T(8,128)(2,1)S(1)}, bf16[256,128]{1,0:T(8,128)(2,1)S(1)}, u32[]{:S(2)}, u32[]{:S(2)}) collective-permute-start(bf16[256,128]{1,0:T(8,128)(2,1)S(1)} %merge.1.here_ref), channel_id=1, source_target_pairs={{0,1},{1,0},{2,3},{3,2},{4,5},{5,4},{6,7},{7,6},{8,9},{9,8},{10,11... | collective-permute-start | bytes 196616 | tf_op jit(solution)/shard_map/ppermute | solution.py:48
  43.8 10.4 %collective-permute-start.17 = (bf16[256,128]{1,0:T(8,128)(2,1)S(1)}, bf16[256,128]{1,0:T(8,128)(2,1)S(1)}, u32[]{:S(2)}, u32[]{:S(2)}) collective-permute-start(bf16[256,128]{1,0:T(8,128)(2,1)S(1)} %collective-permute-done.16.sibling_ref), channel_id=1, source_target_pairs={{0,2},{2,4},{3,1},{4,6},{5,3},{6,8},{7,5},{8,10},{9,7},{10,12},{11... | collective-permute-start | bytes 196616 | tf_op jit(solution)/shard_map/ppermute | solution.py:289
  46.9 7.2 %copy-start.4 = (bf16[128]{0:T(256)(128)(2,1)S(1)}, bf16[128]{0:T(256)(128)(2,1)}, u32[]{:S(2)}) copy-start(bf16[128]{0:T(256)(128)(2,1)} %param.11) | copy-start | bytes 772

commit v2 on v1

--- a/solution.py
+++ b/solution.py
@@ -114,6 +114,25 @@
     )(*queries, *pieces, *state)
 
 
+def join_kernel(*refs):
+    out_ref = refs[-1]
+    for i, ref in enumerate(refs[:-1]):
+        rows = ref.shape[0]
+        out_ref[i * rows : i * rows + rows] = ref[...]
+
+
+def join_call(blocks):
+    rows = sum(block.shape[0] for block in blocks)
+    return pl.pallas_call(
+        join_kernel,
+        out_shape=jax.ShapeDtypeStruct((rows, 128), blocks[0].dtype),
+        in_specs=[VMEM] * len(blocks),
+        out_specs=VMEM,
+        compiler_params=params(),
+        name="join",
+    )(*blocks)
+
+
 def split3(x):
     high = x.astype(jnp.bfloat16)
     rest = x - high.astype(jnp.float32)
@@ -258,7 +277,7 @@
     fence = lax.optimization_barrier
     near = [trade(feat_second, kind, "x", "z") for kind in ("AB", "A", "B")]
     queries = [trade(feat_first, kind, "y") for kind in ("AB", "A", "B")]
-    mine = jnp.concatenate([feat_second] + near, axis=0)
+    mine = join_call([feat_second] + near)
     far_a, far_b, far_ab = [trade(mine, kind, "z", "x") for kind in ("A", "B", "AB")]
     twin = swap(mine)
     query_ab, query_a, query_b = queries
@@ -284,9 +303,8 @@
         feat_first, 0, state, [far_a, far_b, twin_a, twin_b] + tail, scale, packed=False
     )
     mixed = merge_call(feat_first, value_weight, out_weight, own, (from_ab, from_b, from_a))
+    outer = lax.ppermute(mixed, AXES, [(i, i + 1 if i % 2 else i - 1) for i in range(1, 127)])
     sibling = swap(mixed)
-    pairs = [(i, i - 2 if i % 2 else i + 2) for i in range(128)]
-    outer = lax.ppermute(sibling, AXES, [p for p in pairs if 0 <= p[1] < 128])
     rows = near_rows_call(mixed, sibling, conv_weight)
     refined = refine_call(outer, mixed, rows, conv_weight, conv_bias)
     return refined.reshape(1, 256, 128)

time: 55.2 us -> 53.6 us (0.971)
  waiting for transfers between devices: 18.3 us -> 15.5 us
  starting transfers between devices: 20.3 us -> 22.3 us
  Pallas kernels: 15.4 us -> 14.5 us
    ppermute x1, waiting for transfers between devices: 7.22 us -> 4.65 us  [local(): lax.ppermute(mixed, AXES, [(i, i + 1 if i % 2 else i - 1) for i in range(...]
    ppermute x1, starting transfers between devices: 2.84 us -> 4.84 us  [local(): lax.ppermute(mixed, AXES, [(i, i + 1 if i % 2 else i - 1) for i in range(...]
    ppermute x5, waiting for transfers between devices: 1.25 us -> 0.01 us  [swap(): return lax.ppermute(block, AXES, [(i, i ^ 1) for i in range(128)])]
    ppermute x12, waiting for transfers between devices: 9.78 us -> 10.9 us  [trade(): return lax.ppermute(block, AXES, pairs)]
  transfers between devices with their start and end apart: 18 -> 18, of which waited for: 8 -> 7; matrix products, arithmetic and copies ran while one was open for 2% -> 0% of each run, Pallas kernels for 22% -> 21%
where the time goes in v2:
time: 53.6 us; the launch traced here: 53.4 us
  starting transfers between devices  22.3 us (42%)
  waiting for transfers between devices  15.5 us (29%)
  Pallas kernels  14.5 us (27%)
  local copies, waits for them, and re-layouts  0.86 us (2%)
    ppermute x12, starting transfers between devices, trade(): return lax.ppermute(block, AXES, pairs)  16.5 us
    ppermute x12, waiting for transfers between devices, trade(): return lax.ppermute(block, AXES, pairs)  10.9 us
    pallas_call x4, Pallas kernels, keys_call(): pl.pallas_call(functools.partial(keys_kernel, scale, len(queries), len(pi...  6.95 us
    pallas_call x4, Pallas kernels, last_call(): pl.pallas_call(functools.partial(last_kernel, scale, row, len(pieces), pa...  5.9 us
    ppermute x1, starting transfers between devices, local(): lax.ppermute(mixed, AXES, [(i, i + 1 if i % 2 else i - 1) for i in range(...  4.84 us
    ppermute x1, waiting for transfers between devices, local(): lax.ppermute(mixed, AXES, [(i, i + 1 if i % 2 else i - 1) for i in range(...  4.65 us
  transfers between devices with their start and end apart: 18, of which 7 were waited for; matrix products, arithmetic and copies ran while one was open for 0% of the time, Pallas kernels for 21%

profile of v2, /device:TPU:64, one launch (start us, length us, event | category | flops | bytes accessed | tf_op | source)
XLA Modules:
  0.0 53.4 jit_solution(14130863468713208780)
XLA Ops:
  0.0 3.0 %collective-permute-start = (bf16[256,128]{1,0:T(8,128)(2,1)}, bf16[256,128]{1,0:T(8,128)(2,1)S(1)}, u32[]{:S(2)}, u32[]{:S(2)}) collective-permute-start(bf16[256,128]{1,0:T(8,128)(2,1)} %refs_0_.4), channel_id=1, source_target_pairs={{0,32},{1,65},{2,34},{3,67},{4,36},{5,69},{6,38},{7,71},{8,40},{9,... | collective-permute-start | bytes 196616 | tf_op jit(solution)/shard_map/ppermute | solution.py:44
  4.2 1.8 %collective-permute-done.refs_1_ = bf16[256,128]{1,0:T(8,128)(2,1)S(1)} collective-permute-done((bf16[256,128]{1,0:T(8,128)(2,1)}, bf16[256,128]{1,0:T(8,128)(2,1)S(1)}, u32[]{:S(2)}, u32[]{:S(2)}) %collective-permute-start) | collective-permute-done | bytes 65568 | tf_op jit(solution)/shard_map/ppermute | solution.py:44
  6.0 1.5 %collective-permute-done.1.refs_2_ = bf16[256,128]{1,0:T(8,128)(2,1)S(1)} collective-permute-done((bf16[256,128]{1,0:T(8,128)(2,1)}, bf16[256,128]{1,0:T(8,128)(2,1)S(1)}, u32[]{:S(2)}, u32[]{:S(2)}) %collective-permute-start.1) | collective-permute-done | bytes 65568 | tf_op jit(solution)/shard_map/ppermute | solution.py:44
  7.5 1.8 %collective-permute-done.2.refs_3_ = bf16[256,128]{1,0:T(8,128)(2,1)S(1)} collective-permute-done((bf16[256,128]{1,0:T(8,128)(2,1)}, bf16[256,128]{1,0:T(8,128)(2,1)S(1)}, u32[]{:S(2)}, u32[]{:S(2)}) %collective-permute-start.2) | collective-permute-done | bytes 65568 | tf_op jit(solution)/shard_map/ppermute | solution.py:44
  9.3 0.8 %copy-done.2 = bf16[256,128]{1,0:T(8,128)(2,1)S(1)} copy-done((bf16[256,128]{1,0:T(8,128)(2,1)S(1)}, bf16[256,128]{1,0:T(8,128)(2,1)}, u32[]{:S(2)}) %copy-start.2) | copy-done | bytes 65560
  10.3 3.1 %collective-permute-start.6 = (bf16[256,128]{1,0:T(8,128)(2,1)S(1)}, bf16[256,128]{1,0:T(8,128)(2,1)S(1)}, u32[]{:S(2)}, u32[]{:S(2)}) collective-permute-start(bf16[256,128]{1,0:T(8,128)(2,1)S(1)} %copy-done.1), channel_id=1, source_target_pairs={{0,6},{1,7},{2,4},{3,5},{4,2},{5,3},{6,0},{7,1},{8,14},{9,15},{10,... | collective-permute-start | bytes 196616 | tf_op jit(solution)/shard_map/ppermute | solution.py:44
  13.4 1.6 %collective-permute-start.3 = (bf16[1024,128]{1,0:T(8,128)(2,1)S(1)}, bf16[1024,128]{1,0:T(8,128)(2,1)S(1)}, u32[]{:S(2)}, u32[]{:S(2)}) collective-permute-start(bf16[1024,128]{1,0:T(8,128)(2,1)S(1)} %join.1.refs_4_), channel_id=1, source_target_pairs={{0,8},{1,17},{2,10},{3,19},{4,12},{5,21},{6,14},{7,23},{8,0},{9,25... | collective-permute-start | bytes 786440 | tf_op jit(solution)/shard_map/ppermute | solution.py:44
  15.0 0.6 %collective-permute-start.7 = (bf16[256,128]{1,0:T(8,128)(2,1)S(1)}, bf16[256,128]{1,0:T(8,128)(2,1)S(1)}, u32[]{:S(2)}, u32[]{:S(2)}) collective-permute-start(bf16[256,128]{1,0:T(8,128)(2,1)S(1)} %copy-done.1), channel_id=1, source_target_pairs={{0,4},{1,5},{2,6},{3,7},{4,0},{5,1},{6,2},{7,3},{8,12},{9,13},{10,... | collective-permute-start | bytes 196616 | tf_op jit(solution)/shard_map/ppermute | solution.py:44
  16.3 4.6 %collective-permute-done.7.refs_3_.refs_2_.refs_1_.refs_0_ = bf16[256,128]{1,0:T(8,128)(2,1)S(1)} collective-permute-done((bf16[256,128]{1,0:T(8,128)(2,1)S(1)}, bf16[256,128]{1,0:T(8,128)(2,1)S(1)}, u32[]{:S(2)}, u32[]{:S(2)}) %collective-permute-start.7) | collective-permute-done | bytes 65568 | tf_op jit(solution)/shard_map/ppermute | solution.py:44
  21.0 2.3 %collective-permute-start.11 = (bf16[1024,128]{1,0:T(8,128)(2,1)S(1)}, bf16[1024,128]{1,0:T(8,128)(2,1)S(1)}, u32[]{:S(2)}, u32[]{:S(2)}) collective-permute-start(bf16[1024,128]{1,0:T(8,128)(2,1)S(1)} %join.1.refs_4_), channel_id=1, source_target_pairs={{0,64},{1,33},{2,66},{3,35},{4,68},{5,37},{6,70},{7,39},{8,72},{9,... | collective-permute-start | bytes 786440 | tf_op jit(solution)/shard_map/ppermute | solution.py:44
  23.2 1.6 %keys.4 = (f32[1024,128]{1,0:T(8,128)S(1)}, f32[1024,256]{1,0:T(8,128)S(1)}) custom-call(bf16[256,128]{1,0:T(8,128)(2,1)S(1)} %copy-done.1, bf16[256,128]{1,0:T(8,128)(2,1)S(1)} %collective-permute-done.5.refs_1_.refs_0_, bf16[256,128]{1,0:T(8,128)(2,1)S(1)} %collective-permute-done.6.refs_2_.refs_1_.refs_0_, ...), custom_call_target="tpu_custom_call" | custom-call | flops 805306368 | bytes 1048576 | tf_op jit(solution)/shard_map/keys/pallas_call | solution.py:103
  24.8 1.6 %keys.5 = (f32[1024,128]{1,0:T(8,128)S(1)}, f32[1024,256]{1,0:T(8,128)S(1)}) custom-call(bf16[256,128]{1,0:T(8,128)(2,1)S(1)} %copy-done.1, bf16[256,128]{1,0:T(8,128)(2,1)S(1)} %collective-permute-done.5.refs_1_.refs_0_, bf16[256,128]{1,0:T(8,128)(2,1)S(1)} %collective-permute-done.6.refs_2_.refs_1_.refs_0_, ...), custom_call_target="tpu_custom_call" | custom-call | flops 805306368 | bytes 1048576 | tf_op jit(solution)/shard_map/keys/pallas_call | solution.py:103
  27.0 2.2 %keys.6 = (f32[768,128]{1,0:T(8,128)S(1)}, f32[768,256]{1,0:T(8,128)S(1)}) custom-call(bf16[256,128]{1,0:T(8,128)(2,1)S(1)} %collective-permute-done.5.refs_1_.refs_0_, bf16[256,128]{1,0:T(8,128)(2,1)S(1)} %collective-permute-done.6.refs_2_.refs_1_.refs_0_, bf16[256,128]{1,0:T(8,128)(2,1)S(1)} %collective-permute-done.7.refs_3_.refs_2_.refs_1_.refs_0_, ...), custom_call_target="tpu_custom_call" | custom-call | flops 1207959552 | bytes 1048576 | tf_op jit(solution)/shard_map/keys/pallas_call | solution.py:103
  29.4 1.6 %keys.7 = (f32[512,128]{1,0:T(8,128)S(1)}, f32[512,256]{1,0:T(8,128)S(1)}) custom-call(bf16[256,128]{1,0:T(8,128)(2,1)S(1)} %collective-permute-done.6.refs_2_.refs_1_.refs_0_, bf16[256,128]{1,0:T(8,128)(2,1)S(1)} %collective-permute-done.7.refs_3_.refs_2_.refs_1_.refs_0_, bf16[1024,128]{1,0:T(8,128)(2,1)S(1)} %collective-permute-done.9.refs_2_.refs_5_.refs_3_, ...), custom_call_target="tpu_custom_call" | custom-call | flops 805306368 | bytes 1048576 | tf_op jit(solution)/shard_map/keys/pallas_call | solution.py:103
  31.0 1.6 %last_keys.7 = bf16[272,128]{1,0:T(8,128)(2,1)S(1)} custom-call(bf16[256,128]{1,0:T(8,128)(2,1)S(1)} %collective-permute-done.5.refs_1_.refs_0_, f32[768,128]{1,0:T(8,128)S(1)} %get-tuple-element.42.refs_4_.refs_1_, f32[768,256]{1,0:T(8,128)S(1)} %get-tuple-element.43.refs_5_.refs_2_, bf16[1024,128]{1,0:T(8,128)(2,1)S(1)} %collective-permute-done.9.refs_2_.refs_5_.refs_3_, ...), custom_call_target="tpu_custom_call" | custom-call | flops 805306368 | bytes 1048576 | tf_op jit(solution)/shard_map/last_keys/pallas_call | solution.py:198
  33.0 1.0 %last_keys.6 = bf16[272,128]{1,0:T(8,128)(2,1)S(1)} custom-call(bf16[256,128]{1,0:T(8,128)(2,1)S(1)} %collective-permute-done.6.refs_2_.refs_1_.refs_0_, f32[512,128]{1,0:T(8,128)S(1)} %get-tuple-element.49.refs_1_, f32[512,256]{1,0:T(8,128)S(1)} %get-tuple-element.50.refs_2_, bf16[1024,128]{1,0:T(8,128)(2,1)S(1)} %collective-permute-done.11.refs_7_.refs_3_.refs_5_, ...), custom_call_target="tpu_custom_call" | custom-call | flops 402653184 | bytes 1048576 | tf_op jit(solution)/shard_map/last_keys/pallas_call | solution.py:198
  34.1 1.1 %collective-permute-start.14 = (bf16[272,128]{1,0:T(8,128)(2,1)S(1)}, bf16[272,128]{1,0:T(8,128)(2,1)S(1)}, u32[]{:S(2)}, u32[]{:S(2)}) collective-permute-start(bf16[272,128]{1,0:T(8,128)(2,1)S(1)} %last_keys.6), channel_id=1, source_target_pairs={{0,6},{1,7},{2,4},{3,5},{4,2},{5,3},{6,0},{7,1},{8,14},{9,15},{10,... | collective-permute-start | bytes 208904 | tf_op jit(solution)/shard_map/ppermute | solution.py:44
  35.2 1.0 %last_keys.5 = bf16[272,128]{1,0:T(8,128)(2,1)S(1)} custom-call(bf16[256,128]{1,0:T(8,128)(2,1)S(1)} %collective-permute-done.7.refs_3_.refs_2_.refs_1_.refs_0_, f32[512,128]{1,0:T(8,128)S(1)} %get-tuple-element.49.refs_1_, f32[512,256]{1,0:T(8,128)S(1)} %get-tuple-element.50.refs_2_, bf16[1024,128]{1,0:T(8,128)(2,1)S(1)} %collective-permute-done.11.refs_7_.refs_3_.refs_5_, ...), custom_call_target="tpu_custom_call" | custom-call | flops 402653184 | bytes 1048576 | tf_op jit(solution)/shard_map/last_keys/pallas_call | solution.py:198
  36.2 3.0 %collective-permute-start.13 = (bf16[272,128]{1,0:T(8,128)(2,1)S(1)}, bf16[272,128]{1,0:T(8,128)(2,1)S(1)}, u32[]{:S(2)}, u32[]{:S(2)}) collective-permute-start(bf16[272,128]{1,0:T(8,128)(2,1)S(1)} %last_keys.5), channel_id=1, source_target_pairs={{0,4},{1,5},{2,6},{3,7},{4,0},{5,1},{6,2},{7,3},{8,12},{9,13},{10,... | collective-permute-start | bytes 208904 | tf_op jit(solution)/shard_map/ppermute | solution.py:44
  39.2 2.2 %last_keys.4 = (f32[256,128]{1,0:T(8,128)S(1)}, f32[256,256]{1,0:T(8,128)S(1)}) custom-call(bf16[256,128]{1,0:T(8,128)(2,1)S(1)} %copy-done.1, f32[1024,128]{1,0:T(8,128)S(1)} %get-tuple-element.35.refs_5_.refs_1_, f32[1024,256]{1,0:T(8,128)S(1)} %get-tuple-element.36.refs_6_.refs_2_, bf16[1024,128]{1,0:T(8,128)(2,1)S(1)} %collective-permute-done.3.refs_3_, ...), custom_call_target="tpu_custom_call" | custom-call | flops 1207959552 | bytes 1048576 | tf_op jit(solution)/shard_map/last_keys/pallas_call | solution.py:198
  41.4 0.7 %collective-permute-done.13.refs_0_ = bf16[272,128]{1,0:T(8,128)(2,1)S(1)} collective-permute-done((bf16[272,128]{1,0:T(8,128)(2,1)S(1)}, bf16[272,128]{1,0:T(8,128)(2,1)S(1)}, u32[]{:S(2)}, u32[]{:S(2)}) %collective-permute-start.13) | collective-permute-done | bytes 69664 | tf_op jit(solution)/shard_map/ppermute | solution.py:44
  42.7 4.8 %collective-permute-start.16 = (bf16[256,128]{1,0:T(8,128)(2,1)S(1)}, bf16[256,128]{1,0:T(8,128)(2,1)S(1)}, u32[]{:S(2)}, u32[]{:S(2)}) collective-permute-start(bf16[256,128]{1,0:T(8,128)(2,1)S(1)} %merge.1.here_ref), channel_id=1, source_target_pairs={{1,2},{2,1},{3,4},{4,3},{5,6},{6,5},{7,8},{8,7},{9,10},{10,9},{11,... | collective-permute-start | bytes 196616 | tf_op jit(solution)/shard_map/ppermute | solution.py:306
  47.9 4.7 %collective-permute-done.16.outer_ref = bf16[256,128]{1,0:T(8,128)(2,1)S(1)} collective-permute-done((bf16[256,128]{1,0:T(8,128)(2,1)S(1)}, bf16[256,128]{1,0:T(8,128)(2,1)S(1)}, u32[]{:S(2)}, u32[]{:S(2)}) %collective-permute-start.16) | collective-permute-done | bytes 65568 | tf_op jit(solution)/shard_map/ppermute | solution.py:306
  52.5 0.9 %refine.1 = bf16[256,128]{1,0:T(8,128)(2,1)} custom-call(bf16[256,128]{1,0:T(8,128)(2,1)S(1)} %collective-permute-done.16.outer_ref, bf16[256,128]{1,0:T(8,128)(2,1)S(1)} %merge.1.here_ref, f32[256,384]{1,0:T(8,128)S(1)} %near_rows.1.near_ref, bf16[3,3,128,128]{3,2,1,0:T(8,128)(2,1)S(1)} %copy-done, bf16[1,128]{1,0:T(2,128)(2,1)S(1)} %bitcast.2), custom_call_target="tpu_custom_call" | custom-call | tf_op jit(solution)/shard_map/refine/pallas_call | solution.py:265
  (36 shorter events, 3.9 us)
Async XLA Ops:
  0.0 10.3 %copy-start.1 = (bf16[256,128]{1,0:T(8,128)(2,1)S(1)}, bf16[256,128]{1,0:T(8,128)(2,1)}, u32[]{:S(2)}) copy-start(bf16[256,128]{1,0:T(8,128)(2,1)} %q_ref.1) | copy-start | bytes 196612
  0.0 6.0 %collective-permute-start = (bf16[256,128]{1,0:T(8,128)(2,1)}, bf16[256,128]{1,0:T(8,128)(2,1)S(1)}, u32[]{:S(2)}, u32[]{:S(2)}) collective-permute-start(bf16[256,128]{1,0:T(8,128)(2,1)} %refs_0_.4), channel_id=1, source_target_pairs={{0,32},{1,65},{2,34},{3,67},{4,36},{5,69},{6,38},{7,71},{8,40},{9,... | collective-permute-start | bytes 196616 | tf_op jit(solution)/shard_map/ppermute | solution.py:44
  3.0 4.5 %collective-permute-start.1 = (bf16[256,128]{1,0:T(8,128)(2,1)}, bf16[256,128]{1,0:T(8,128)(2,1)S(1)}, u32[]{:S(2)}, u32[]{:S(2)}) collective-permute-start(bf16[256,128]{1,0:T(8,128)(2,1)} %refs_0_.4), channel_id=1, source_target_pairs={{0,16},{1,9},{2,18},{3,11},{4,20},{5,13},{6,22},{7,15},{8,24},{9,1... | collective-permute-start | bytes 196616 | tf_op jit(solution)/shard_map/ppermute | solution.py:44
  3.6 5.7 %collective-permute-start.2 = (bf16[256,128]{1,0:T(8,128)(2,1)}, bf16[256,128]{1,0:T(8,128)(2,1)S(1)}, u32[]{:S(2)}, u32[]{:S(2)}) collective-permute-start(bf16[256,128]{1,0:T(8,128)(2,1)} %refs_0_.4), channel_id=1, source_target_pairs={{0,48},{1,73},{2,50},{3,75},{4,52},{5,77},{6,54},{7,79},{8,56},{9,... | collective-permute-start | bytes 196616 | tf_op jit(solution)/shard_map/ppermute | solution.py:44
  9.3 0.8 %copy-start.2 = (bf16[256,128]{1,0:T(8,128)(2,1)S(1)}, bf16[256,128]{1,0:T(8,128)(2,1)}, u32[]{:S(2)}) copy-start(bf16[256,128]{1,0:T(8,128)(2,1)} %refs_0_.4) | copy-start | bytes 196612
  10.2 14.6 %collective-permute-start.8 = (bf16[1024,128]{1,0:T(8,128)(2,1)S(1)}, bf16[1024,128]{1,0:T(8,128)(2,1)S(1)}, u32[]{:S(2)}, u32[]{:S(2)}) collective-permute-start(bf16[1024,128]{1,0:T(8,128)(2,1)S(1)} %join.1.refs_4_), channel_id=1, source_target_pairs={{0,1},{1,0},{2,3},{3,2},{4,5},{5,4},{6,7},{7,6},{8,9},{9,8},{10,11... | collective-permute-start | bytes 786440 | tf_op jit(solution)/shard_map/ppermute | solution.py:48
  10.3 5.8 %collective-permute-start.6 = (bf16[256,128]{1,0:T(8,128)(2,1)S(1)}, bf16[256,128]{1,0:T(8,128)(2,1)S(1)}, u32[]{:S(2)}, u32[]{:S(2)}) collective-permute-start(bf16[256,128]{1,0:T(8,128)(2,1)S(1)} %copy-done.1), channel_id=1, source_target_pairs={{0,6},{1,7},{2,4},{3,5},{4,2},{5,3},{6,0},{7,1},{8,14},{9,15},{10,... | collective-permute-start | bytes 196616 | tf_op jit(solution)/shard_map/ppermute | solution.py:44
  13.4 13.1 %collective-permute-start.3 = (bf16[1024,128]{1,0:T(8,128)(2,1)S(1)}, bf16[1024,128]{1,0:T(8,128)(2,1)S(1)}, u32[]{:S(2)}, u32[]{:S(2)}) collective-permute-start(bf16[1024,128]{1,0:T(8,128)(2,1)S(1)} %join.1.refs_4_), channel_id=1, source_target_pairs={{0,8},{1,17},{2,10},{3,19},{4,12},{5,21},{6,14},{7,23},{8,0},{9,25... | collective-permute-start | bytes 786440 | tf_op jit(solution)/shard_map/ppermute | solution.py:44
  15.0 11.4 %collective-permute-start.4 = (bf16[1024,128]{1,0:T(8,128)(2,1)S(1)}, bf16[1024,128]{1,0:T(8,128)(2,1)S(1)}, u32[]{:S(2)}, u32[]{:S(2)}) collective-permute-start(bf16[1024,128]{1,0:T(8,128)(2,1)S(1)} %join.1.refs_4_), channel_id=1, source_target_pairs={{0,72},{1,49},{2,74},{3,51},{4,76},{5,53},{6,78},{7,55},{8,64},{9,... | collective-permute-start | bytes 786440 | tf_op jit(solution)/shard_map/ppermute | solution.py:44
  15.0 6.0 %collective-permute-start.7 = (bf16[256,128]{1,0:T(8,128)(2,1)S(1)}, bf16[256,128]{1,0:T(8,128)(2,1)S(1)}, u32[]{:S(2)}, u32[]{:S(2)}) collective-permute-start(bf16[256,128]{1,0:T(8,128)(2,1)S(1)} %copy-done.1), channel_id=1, source_target_pairs={{0,4},{1,5},{2,6},{3,7},{4,0},{5,1},{6,2},{7,3},{8,12},{9,13},{10,... | collective-permute-start | bytes 196616 | tf_op jit(solution)/shard_map/ppermute | solution.py:44
  16.0 7.2 %collective-permute-start.5 = (bf16[256,128]{1,0:T(8,128)(2,1)S(1)}, bf16[256,128]{1,0:T(8,128)(2,1)S(1)}, u32[]{:S(2)}, u32[]{:S(2)}) collective-permute-start(bf16[256,128]{1,0:T(8,128)(2,1)S(1)} %copy-done.1), channel_id=1, source_target_pairs={{0,2},{1,3},{2,0},{3,1},{4,6},{5,7},{6,4},{7,5},{8,10},{9,11},{10,... | collective-permute-start | bytes 196616 | tf_op jit(solution)/shard_map/ppermute | solution.py:44
  21.0 8.3 %collective-permute-start.11 = (bf16[1024,128]{1,0:T(8,128)(2,1)S(1)}, bf16[1024,128]{1,0:T(8,128)(2,1)S(1)}, u32[]{:S(2)}, u32[]{:S(2)}) collective-permute-start(bf16[1024,128]{1,0:T(8,128)(2,1)S(1)} %join.1.refs_4_), channel_id=1, source_target_pairs={{0,64},{1,33},{2,66},{3,35},{4,68},{5,37},{6,70},{7,39},{8,72},{9,... | collective-permute-start | bytes 786440 | tf_op jit(solution)/shard_map/ppermute | solution.py:44
  26.4 3.0 %collective-permute-start.10 = (bf16[1024,128]{1,0:T(8,128)(2,1)S(1)}, bf16[1024,128]{1,0:T(8,128)(2,1)S(1)}, u32[]{:S(2)}, u32[]{:S(2)}) collective-permute-start(bf16[1024,128]{1,0:T(8,128)(2,1)S(1)} %collective-permute-done.4.refs_4_), channel_id=1, source_target_pairs={{0,1},{1,0},{2,3},{3,2},{4,5},{5,4},{6,7},{7,6},{8,9},{9,8},{10,11... | collective-permute-start | bytes 786440 | tf_op jit(solution)/shard_map/ppermute | solution.py:48
  26.5 2.9 %collective-permute-start.9 = (bf16[1024,128]{1,0:T(8,128)(2,1)S(1)}, bf16[1024,128]{1,0:T(8,128)(2,1)S(1)}, u32[]{:S(2)}, u32[]{:S(2)}) collective-permute-start(bf16[1024,128]{1,0:T(8,128)(2,1)S(1)} %collective-permute-done.3.refs_3_), channel_id=1, source_target_pairs={{0,1},{1,0},{2,3},{3,2},{4,5},{5,4},{6,7},{7,6},{8,9},{9,8},{10,11... | collective-permute-start | bytes 786440 | tf_op jit(solution)/shard_map/ppermute | solution.py:48
  29.3 1.8 %collective-permute-start.12 = (bf16[1024,128]{1,0:T(8,128)(2,1)S(1)}, bf16[1024,128]{1,0:T(8,128)(2,1)S(1)}, u32[]{:S(2)}, u32[]{:S(2)}) collective-permute-start(bf16[1024,128]{1,0:T(8,128)(2,1)S(1)} %collective-permute-done.11.refs_7_.refs_3_.refs_5_), channel_id=1, source_target_pairs={{0,1},{1,0},{2,3},{3,2},{4,5},{5,4},{6,7},{7,6},{8,9},{9,8},{10,11... | collective-permute-start | bytes 786440 | tf_op jit(solution)/shard_map/ppermute | solution.py:48
  32.7 8.7 %collective-permute-start.15 = (bf16[272,128]{1,0:T(8,128)(2,1)S(1)}, bf16[272,128]{1,0:T(8,128)(2,1)S(1)}, u32[]{:S(2)}, u32[]{:S(2)}) collective-permute-start(bf16[272,128]{1,0:T(8,128)(2,1)S(1)} %last_keys.7), channel_id=1, source_target_pairs={{0,2},{1,3},{2,0},{3,1},{4,6},{5,7},{6,4},{7,5},{8,10},{9,11},{10,... | collective-permute-start | bytes 208904 | tf_op jit(solution)/shard_map/ppermute | solution.py:44
  34.1 7.3 %collective-permute-start.14 = (bf16[272,128]{1,0:T(8,128)(2,1)S(1)}, bf16[272,128]{1,0:T(8,128)(2,1)S(1)}, u32[]{:S(2)}, u32[]{:S(2)}) collective-permute-start(bf16[272,128]{1,0:T(8,128)(2,1)S(1)} %last_keys.6), channel_id=1, source_target_pairs={{0,6},{1,7},{2,4},{3,5},{4,2},{5,3},{6,0},{7,1},{8,14},{9,15},{10,... | collective-permute-start | bytes 208904 | tf_op jit(solution)/shard_map/ppermute | solution.py:44
  36.2 5.9 %copy-start.3 = (bf16[128,128]{1,0:T(8,128)(2,1)S(1)}, bf16[128,128]{1,0:T(8,128)(2,1)}, u32[]{:S(2)}) copy-start(bf16[128,128]{1,0:T(8,128)(2,1)} %vw_ref.1) | copy-start | bytes 98308
  36.2 5.9 %copy-start.4 = (bf16[128,128]{1,0:T(8,128)(2,1)S(1)}, bf16[128,128]{1,0:T(8,128)(2,1)}, u32[]{:S(2)}) copy-start(bf16[128,128]{1,0:T(8,128)(2,1)} %ow_ref.1) | copy-start | bytes 98308
  36.2 5.9 %collective-permute-start.13 = (bf16[272,128]{1,0:T(8,128)(2,1)S(1)}, bf16[272,128]{1,0:T(8,128)(2,1)S(1)}, u32[]{:S(2)}, u32[]{:S(2)}) collective-permute-start(bf16[272,128]{1,0:T(8,128)(2,1)S(1)} %last_keys.5), channel_id=1, source_target_pairs={{0,4},{1,5},{2,6},{3,7},{4,0},{5,1},{6,2},{7,3},{8,12},{9,13},{10,... | collective-permute-start | bytes 208904 | tf_op jit(solution)/shard_map/ppermute | solution.py:44
  42.1 5.4 %copy-start = (bf16[3,3,128,128]{3,2,1,0:T(8,128)(2,1)S(1)}, bf16[3,3,128,128]{3,2,1,0:T(8,128)(2,1)}, u32[]{:S(2)}) copy-start(bf16[3,3,128,128]{3,2,1,0:T(8,128)(2,1)} %w_ref.3) | copy-start | bytes 884740
  42.6 4.9 %collective-permute-start.17 = (bf16[256,128]{1,0:T(8,128)(2,1)S(1)}, bf16[256,128]{1,0:T(8,128)(2,1)S(1)}, u32[]{:S(2)}, u32[]{:S(2)}) collective-permute-start(bf16[256,128]{1,0:T(8,128)(2,1)S(1)} %merge.1.here_ref), channel_id=1, source_target_pairs={{0,1},{1,0},{2,3},{3,2},{4,5},{5,4},{6,7},{7,6},{8,9},{9,8},{10,11... | collective-permute-start | bytes 196616 | tf_op jit(solution)/shard_map/ppermute | solution.py:48
  42.7 9.8 %collective-permute-start.16 = (bf16[256,128]{1,0:T(8,128)(2,1)S(1)}, bf16[256,128]{1,0:T(8,128)(2,1)S(1)}, u32[]{:S(2)}, u32[]{:S(2)}) collective-permute-start(bf16[256,128]{1,0:T(8,128)(2,1)S(1)} %merge.1.here_ref), channel_id=1, source_target_pairs={{1,2},{2,1},{3,4},{4,3},{5,6},{6,5},{7,8},{8,7},{9,10},{10,9},{11,... | collective-permute-start | bytes 196616 | tf_op jit(solution)/shard_map/ppermute | solution.py:306
  47.8 4.7 %copy-start.5 = (bf16[128]{0:T(256)(128)(2,1)S(1)}, bf16[128]{0:T(256)(128)(2,1)}, u32[]{:S(2)}) copy-start(bf16[128]{0:T(256)(128)(2,1)} %param.11) | copy-start | bytes 772

commit v3 on v2

--- a/solution.py
+++ b/solution.py
@@ -114,23 +114,38 @@
     )(*queries, *pieces, *state)
 
 
-def join_kernel(*refs):
+def stage_kernel(own_ref, out_ref):
+    out_ref[0 : own_ref.shape[0]] = own_ref[...]
+
+
+def join_kernel(staged_ref, *refs):
     out_ref = refs[-1]
     for i, ref in enumerate(refs[:-1]):
         rows = ref.shape[0]
-        out_ref[i * rows : i * rows + rows] = ref[...]
-
-
-def join_call(blocks):
-    rows = sum(block.shape[0] for block in blocks)
+        out_ref[(i + 1) * rows : (i + 2) * rows] = ref[...]
+
+
+def stage_call(own, count):
+    return pl.pallas_call(
+        stage_kernel,
+        out_shape=jax.ShapeDtypeStruct((own.shape[0] * count, 128), own.dtype),
+        in_specs=[VMEM],
+        out_specs=VMEM,
+        compiler_params=params(),
+        name="stage",
+    )(own)
+
+
+def join_call(staged, blocks):
     return pl.pallas_call(
         join_kernel,
-        out_shape=jax.ShapeDtypeStruct((rows, 128), blocks[0].dtype),
-        in_specs=[VMEM] * len(blocks),
-        out_specs=VMEM,
+        out_shape=jax.ShapeDtypeStruct(staged.shape, staged.dtype),
+        in_specs=[VMEM] * (1 + len(blocks)),
+        out_specs=VMEM,
+        input_output_aliases={0: 0},
         compiler_params=params(),
         name="join",
-    )(*blocks)
+    )(staged, *blocks)
 
 
 def split3(x):
@@ -235,41 +250,44 @@
     return jnp.dot(row_ref[...], taps, preferred_element_type=jnp.float32)
 
 
-def near_rows_kernel(here_ref, sibling_ref, w_ref, out_ref):
+def near_rows_kernel(here_ref, sibling_ref, w_ref, bias_ref, out_ref):
     odd = lax.axis_index("ka") % 2
-    out_ref[...] = taps_of(here_ref, w_ref, 1) + taps_of(sibling_ref, w_ref, 2 - 2 * odd)
-
-
-def refine_kernel(outer_ref, here_ref, near_ref, w_ref, bias_ref, out_ref):
+    total = taps_of(here_ref, w_ref, 1) + taps_of(sibling_ref, w_ref, 2 - 2 * odd)
+    out_ref[:, 0:128] = total[:, 0:128]
+    out_ref[:, 128:256] = total[:, 128:256] + bias_ref[...].astype(jnp.float32)
+    out_ref[:, 256:384] = total[:, 256:384]
+
+
+def refine_kernel(outer_ref, here_ref, near_ref, w_ref, out_ref):
     odd = lax.axis_index("ka") % 2
     total = near_ref[...] + taps_of(outer_ref, w_ref, 2 * odd)
     at = lax.broadcasted_iota(jnp.int32, (256, 128), 0)
     left = jnp.where(at == 0, 0.0, pltpu.roll(total[:, 0:128], 1, 0))
     right = jnp.where(at == 255, 0.0, pltpu.roll(total[:, 256:384], 255, 0))
-    conv = left + total[:, 128:256] + right + bias_ref[...].astype(jnp.float32)
+    conv = left + total[:, 128:256] + right
     out_ref[...] = (here_ref[...].astype(jnp.float32) + jax.nn.gelu(conv)).astype(jnp.bfloat16)
 
 
-def near_rows_call(here, sibling, w):
+def near_rows_call(here, sibling, w, bias):
     return pl.pallas_call(
         near_rows_kernel,
         out_shape=jax.ShapeDtypeStruct((256, 384), jnp.float32),
-        in_specs=[VMEM] * 3,
+        in_specs=[VMEM] * 4,
         out_specs=VMEM,
         compiler_params=params(),
         name="near_rows",
-    )(here, sibling, w)
-
-
-def refine_call(outer, here, near, w, bias):
+    )(here, sibling, w, bias.reshape(1, 128))
+
+
+def refine_call(outer, here, near, w):
     return pl.pallas_call(
         refine_kernel,
         out_shape=jax.ShapeDtypeStruct((256, 128), jnp.bfloat16),
-        in_specs=[VMEM] * 5,
+        in_specs=[VMEM] * 4,
         out_specs=VMEM,
         compiler_params=params(),
         name="refine",
-    )(outer, here, near, w, bias.reshape(1, 128))
+    )(outer, here, near, w)
 
 
 def local(feat_first, feat_second, value_weight, out_weight, conv_weight, conv_bias):
@@ -277,7 +295,7 @@
     fence = lax.optimization_barrier
     near = [trade(feat_second, kind, "x", "z") for kind in ("AB", "A", "B")]
     queries = [trade(feat_first, kind, "y") for kind in ("AB", "A", "B")]
-    mine = join_call([feat_second] + near)
+    mine = join_call(stage_call(feat_second, 4), near)
     far_a, far_b, far_ab = [trade(mine, kind, "z", "x") for kind in ("A", "B", "AB")]
     twin = swap(mine)
     query_ab, query_a, query_b = queries
@@ -305,8 +323,8 @@
     mixed = merge_call(feat_first, value_weight, out_weight, own, (from_ab, from_b, from_a))
     outer = lax.ppermute(mixed, AXES, [(i, i + 1 if i % 2 else i - 1) for i in range(1, 127)])
     sibling = swap(mixed)
-    rows = near_rows_call(mixed, sibling, conv_weight)
-    refined = refine_call(outer, mixed, rows, conv_weight, conv_bias)
+    rows = near_rows_call(mixed, sibling, conv_weight, conv_bias)
+    refined = refine_call(outer, mixed, rows, conv_weight)
     return refined.reshape(1, 256, 128)
 
 

time: 53.6 us -> 52.7 us (0.983)
  waiting for transfers between devices: 15.5 us -> 14.7 us
    ppermute x12, waiting for transfers between devices: 10.9 us -> 10 us  [trade(): return lax.ppermute(block, AXES, pairs)]
  transfers between devices with their start and end apart: 18 -> 18, of which waited for: 7 -> 7; matrix products, arithmetic and copies ran while one was open for 0% -> 0% of each run, Pallas kernels for 21% -> 22%
where the time goes in v3:
time: 52.7 us; the launch traced here: 52.6 us
  starting transfers between devices  22.3 us (42%)
  waiting for transfers between devices  14.7 us (28%)
  Pallas kernels  14.5 us (28%)
  local copies, waits for them, and re-layouts  0.89 us (2%)
    ppermute x12, starting transfers between devices, trade(): return lax.ppermute(block, AXES, pairs)  16.5 us
    ppermute x12, waiting for transfers between devices, trade(): return lax.ppermute(block, AXES, pairs)  10 us
    pallas_call x4, Pallas kernels, keys_call(): pl.pallas_call(functools.partial(keys_kernel, scale, len(queries), len(pi...  6.95 us
    pallas_call x4, Pallas kernels, last_call(): pl.pallas_call(functools.partial(last_kernel, scale, row, len(pieces), pa...  5.9 us
    ppermute x1, starting transfers between devices, local(): lax.ppermute(mixed, AXES, [(i, i + 1 if i % 2 else i - 1) for i in range(...  4.85 us
    ppermute x1, waiting for transfers between devices, local(): lax.ppermute(mixed, AXES, [(i, i + 1 if i % 2 else i - 1) for i in range(...  4.65 us
  transfers between devices with their start and end apart: 18, of which 7 were waited for; matrix products, arithmetic and copies ran while one was open for 0% of the time, Pallas kernels for 22%

profile of v3, /device:TPU:64, one launch (start us, length us, event | category | flops | bytes accessed | tf_op | source)
XLA Modules:
  0.0 52.6 jit_solution(2020364707844639431)
XLA Ops:
  0.0 3.0 %collective-permute-start = (bf16[256,128]{1,0:T(8,128)(2,1)}, bf16[256,128]{1,0:T(8,128)(2,1)S(1)}, u32[]{:S(2)}, u32[]{:S(2)}) collective-permute-start(bf16[256,128]{1,0:T(8,128)(2,1)} %own_ref.1), channel_id=1, source_target_pairs={{0,32},{1,65},{2,34},{3,67},{4,36},{5,69},{6,38},{7,71},{8,40},{9,... | collective-permute-start | bytes 196616 | tf_op jit(solution)/shard_map/ppermute | solution.py:44
  4.2 0.9 %copy-done.1 = bf16[256,128]{1,0:T(8,128)(2,1)S(1)} copy-done((bf16[256,128]{1,0:T(8,128)(2,1)S(1)}, bf16[256,128]{1,0:T(8,128)(2,1)}, u32[]{:S(2)}) %copy-start.1) | copy-done | bytes 65560
  5.0 0.9 %collective-permute-done.refs_0_ = bf16[256,128]{1,0:T(8,128)(2,1)S(1)} collective-permute-done((bf16[256,128]{1,0:T(8,128)(2,1)}, bf16[256,128]{1,0:T(8,128)(2,1)S(1)}, u32[]{:S(2)}, u32[]{:S(2)}) %collective-permute-start) | collective-permute-done | bytes 65568 | tf_op jit(solution)/shard_map/ppermute | solution.py:44
  6.0 1.5 %collective-permute-done.1.refs_1_ = bf16[256,128]{1,0:T(8,128)(2,1)S(1)} collective-permute-done((bf16[256,128]{1,0:T(8,128)(2,1)}, bf16[256,128]{1,0:T(8,128)(2,1)S(1)}, u32[]{:S(2)}, u32[]{:S(2)}) %collective-permute-start.1) | collective-permute-done | bytes 65568 | tf_op jit(solution)/shard_map/ppermute | solution.py:44
  7.5 1.8 %collective-permute-done.2.refs_2_ = bf16[256,128]{1,0:T(8,128)(2,1)S(1)} collective-permute-done((bf16[256,128]{1,0:T(8,128)(2,1)}, bf16[256,128]{1,0:T(8,128)(2,1)S(1)}, u32[]{:S(2)}, u32[]{:S(2)}) %collective-permute-start.2) | collective-permute-done | bytes 65568 | tf_op jit(solution)/shard_map/ppermute | solution.py:44
  9.4 3.1 %collective-permute-start.6 = (bf16[256,128]{1,0:T(8,128)(2,1)S(1)}, bf16[256,128]{1,0:T(8,128)(2,1)S(1)}, u32[]{:S(2)}, u32[]{:S(2)}) collective-permute-start(bf16[256,128]{1,0:T(8,128)(2,1)S(1)} %copy-done.2), channel_id=1, source_target_pairs={{0,6},{1,7},{2,4},{3,5},{4,2},{5,3},{6,0},{7,1},{8,14},{9,15},{10,... | collective-permute-start | bytes 196616 | tf_op jit(solution)/shard_map/ppermute | solution.py:44
  12.5 1.6 %collective-permute-start.3 = (bf16[1024,128]{1,0:T(8,128)(2,1)S(1)}, bf16[1024,128]{1,0:T(8,128)(2,1)S(1)}, u32[]{:S(2)}, u32[]{:S(2)}) collective-permute-start(bf16[1024,128]{1,0:T(8,128)(2,1)S(1)} %join.1.refs_4_), channel_id=1, source_target_pairs={{0,8},{1,17},{2,10},{3,19},{4,12},{5,21},{6,14},{7,23},{8,0},{9,25... | collective-permute-start | bytes 786440 | tf_op jit(solution)/shard_map/ppermute | solution.py:44
  14.1 0.6 %collective-permute-start.7 = (bf16[256,128]{1,0:T(8,128)(2,1)S(1)}, bf16[256,128]{1,0:T(8,128)(2,1)S(1)}, u32[]{:S(2)}, u32[]{:S(2)}) collective-permute-start(bf16[256,128]{1,0:T(8,128)(2,1)S(1)} %copy-done.2), channel_id=1, source_target_pairs={{0,4},{1,5},{2,6},{3,7},{4,0},{5,1},{6,2},{7,3},{8,12},{9,13},{10,... | collective-permute-start | bytes 196616 | tf_op jit(solution)/shard_map/ppermute | solution.py:44
  15.5 4.6 %collective-permute-done.7.refs_3_.refs_2_.refs_1_.refs_0_ = bf16[256,128]{1,0:T(8,128)(2,1)S(1)} collective-permute-done((bf16[256,128]{1,0:T(8,128)(2,1)S(1)}, bf16[256,128]{1,0:T(8,128)(2,1)S(1)}, u32[]{:S(2)}, u32[]{:S(2)}) %collective-permute-start.7) | collective-permute-done | bytes 65568 | tf_op jit(solution)/shard_map/ppermute | solution.py:44
  20.1 2.3 %collective-permute-start.11 = (bf16[1024,128]{1,0:T(8,128)(2,1)S(1)}, bf16[1024,128]{1,0:T(8,128)(2,1)S(1)}, u32[]{:S(2)}, u32[]{:S(2)}) collective-permute-start(bf16[1024,128]{1,0:T(8,128)(2,1)S(1)} %join.1.refs_4_), channel_id=1, source_target_pairs={{0,64},{1,33},{2,66},{3,35},{4,68},{5,37},{6,70},{7,39},{8,72},{9,... | collective-permute-start | bytes 786440 | tf_op jit(solution)/shard_map/ppermute | solution.py:44
  22.4 1.6 %keys.4 = (f32[1024,128]{1,0:T(8,128)S(1)}, f32[1024,256]{1,0:T(8,128)S(1)}) custom-call(bf16[256,128]{1,0:T(8,128)(2,1)S(1)} %copy-done.2, bf16[256,128]{1,0:T(8,128)(2,1)S(1)} %collective-permute-done.5.refs_1_.refs_0_, bf16[256,128]{1,0:T(8,128)(2,1)S(1)} %collective-permute-done.6.refs_2_.refs_1_.refs_0_, ...), custom_call_target="tpu_custom_call" | custom-call | flops 805306368 | bytes 1048576 | tf_op jit(solution)/shard_map/keys/pallas_call | solution.py:103
  24.0 1.6 %keys.5 = (f32[1024,128]{1,0:T(8,128)S(1)}, f32[1024,256]{1,0:T(8,128)S(1)}) custom-call(bf16[256,128]{1,0:T(8,128)(2,1)S(1)} %copy-done.2, bf16[256,128]{1,0:T(8,128)(2,1)S(1)} %collective-permute-done.5.refs_1_.refs_0_, bf16[256,128]{1,0:T(8,128)(2,1)S(1)} %collective-permute-done.6.refs_2_.refs_1_.refs_0_, ...), custom_call_target="tpu_custom_call" | custom-call | flops 805306368 | bytes 1048576 | tf_op jit(solution)/shard_map/keys/pallas_call | solution.py:103
  26.2 2.2 %keys.6 = (f32[768,128]{1,0:T(8,128)S(1)}, f32[768,256]{1,0:T(8,128)S(1)}) custom-call(bf16[256,128]{1,0:T(8,128)(2,1)S(1)} %collective-permute-done.5.refs_1_.refs_0_, bf16[256,128]{1,0:T(8,128)(2,1)S(1)} %collective-permute-done.6.refs_2_.refs_1_.refs_0_, bf16[256,128]{1,0:T(8,128)(2,1)S(1)} %collective-permute-done.7.refs_3_.refs_2_.refs_1_.refs_0_, ...), custom_call_target="tpu_custom_call" | custom-call | flops 1207959552 | bytes 1048576 | tf_op jit(solution)/shard_map/keys/pallas_call | solution.py:103
  28.6 1.6 %keys.7 = (f32[512,128]{1,0:T(8,128)S(1)}, f32[512,256]{1,0:T(8,128)S(1)}) custom-call(bf16[256,128]{1,0:T(8,128)(2,1)S(1)} %collective-permute-done.6.refs_2_.refs_1_.refs_0_, bf16[256,128]{1,0:T(8,128)(2,1)S(1)} %collective-permute-done.7.refs_3_.refs_2_.refs_1_.refs_0_, bf16[1024,128]{1,0:T(8,128)(2,1)S(1)} %collective-permute-done.9.refs_2_.refs_5_.refs_3_, ...), custom_call_target="tpu_custom_call" | custom-call | flops 805306368 | bytes 1048576 | tf_op jit(solution)/shard_map/keys/pallas_call | solution.py:103
  30.2 1.6 %last_keys.7 = bf16[272,128]{1,0:T(8,128)(2,1)S(1)} custom-call(bf16[256,128]{1,0:T(8,128)(2,1)S(1)} %collective-permute-done.5.refs_1_.refs_0_, f32[768,128]{1,0:T(8,128)S(1)} %get-tuple-element.42.refs_4_.refs_1_, f32[768,256]{1,0:T(8,128)S(1)} %get-tuple-element.43.refs_5_.refs_2_, bf16[1024,128]{1,0:T(8,128)(2,1)S(1)} %collective-permute-done.9.refs_2_.refs_5_.refs_3_, ...), custom_call_target="tpu_custom_call" | custom-call | flops 805306368 | bytes 1048576 | tf_op jit(solution)/shard_map/last_keys/pallas_call | solution.py:213
  32.2 1.0 %last_keys.6 = bf16[272,128]{1,0:T(8,128)(2,1)S(1)} custom-call(bf16[256,128]{1,0:T(8,128)(2,1)S(1)} %collective-permute-done.6.refs_2_.refs_1_.refs_0_, f32[512,128]{1,0:T(8,128)S(1)} %get-tuple-element.49.refs_1_, f32[512,256]{1,0:T(8,128)S(1)} %get-tuple-element.50.refs_2_, bf16[1024,128]{1,0:T(8,128)(2,1)S(1)} %collective-permute-done.11.refs_7_.refs_3_.refs_5_, ...), custom_call_target="tpu_custom_call" | custom-call | flops 402653184 | bytes 1048576 | tf_op jit(solution)/shard_map/last_keys/pallas_call | solution.py:213
  33.2 1.1 %collective-permute-start.14 = (bf16[272,128]{1,0:T(8,128)(2,1)S(1)}, bf16[272,128]{1,0:T(8,128)(2,1)S(1)}, u32[]{:S(2)}, u32[]{:S(2)}) collective-permute-start(bf16[272,128]{1,0:T(8,128)(2,1)S(1)} %last_keys.6), channel_id=1, source_target_pairs={{0,6},{1,7},{2,4},{3,5},{4,2},{5,3},{6,0},{7,1},{8,14},{9,15},{10,... | collective-permute-start | bytes 208904 | tf_op jit(solution)/shard_map/ppermute | solution.py:44
  34.3 1.0 %last_keys.5 = bf16[272,128]{1,0:T(8,128)(2,1)S(1)} custom-call(bf16[256,128]{1,0:T(8,128)(2,1)S(1)} %collective-permute-done.7.refs_3_.refs_2_.refs_1_.refs_0_, f32[512,128]{1,0:T(8,128)S(1)} %get-tuple-element.49.refs_1_, f32[512,256]{1,0:T(8,128)S(1)} %get-tuple-element.50.refs_2_, bf16[1024,128]{1,0:T(8,128)(2,1)S(1)} %collective-permute-done.11.refs_7_.refs_3_.refs_5_, ...), custom_call_target="tpu_custom_call" | custom-call | flops 402653184 | bytes 1048576 | tf_op jit(solution)/shard_map/last_keys/pallas_call | solution.py:213
  35.4 3.0 %collective-permute-start.13 = (bf16[272,128]{1,0:T(8,128)(2,1)S(1)}, bf16[272,128]{1,0:T(8,128)(2,1)S(1)}, u32[]{:S(2)}, u32[]{:S(2)}) collective-permute-start(bf16[272,128]{1,0:T(8,128)(2,1)S(1)} %last_keys.5), channel_id=1, source_target_pairs={{0,4},{1,5},{2,6},{3,7},{4,0},{5,1},{6,2},{7,3},{8,12},{9,13},{10,... | collective-permute-start | bytes 208904 | tf_op jit(solution)/shard_map/ppermute | solution.py:44
  38.4 2.2 %last_keys.4 = (f32[256,128]{1,0:T(8,128)S(1)}, f32[256,256]{1,0:T(8,128)S(1)}) custom-call(bf16[256,128]{1,0:T(8,128)(2,1)S(1)} %copy-done.2, f32[1024,128]{1,0:T(8,128)S(1)} %get-tuple-element.35.refs_5_.refs_1_, f32[1024,256]{1,0:T(8,128)S(1)} %get-tuple-element.36.refs_6_.refs_2_, bf16[1024,128]{1,0:T(8,128)(2,1)S(1)} %collective-permute-done.3.refs_3_, ...), custom_call_target="tpu_custom_call" | custom-call | flops 1207959552 | bytes 1048576 | tf_op jit(solution)/shard_map/last_keys/pallas_call | solution.py:213
  40.6 0.7 %collective-permute-done.13.refs_0_ = bf16[272,128]{1,0:T(8,128)(2,1)S(1)} collective-permute-done((bf16[272,128]{1,0:T(8,128)(2,1)S(1)}, bf16[272,128]{1,0:T(8,128)(2,1)S(1)}, u32[]{:S(2)}, u32[]{:S(2)}) %collective-permute-start.13) | collective-permute-done | bytes 69664 | tf_op jit(solution)/shard_map/ppermute | solution.py:44
  41.9 4.8 %collective-permute-start.16 = (bf16[256,128]{1,0:T(8,128)(2,1)S(1)}, bf16[256,128]{1,0:T(8,128)(2,1)S(1)}, u32[]{:S(2)}, u32[]{:S(2)}) collective-permute-start(bf16[256,128]{1,0:T(8,128)(2,1)S(1)} %merge.1.here_ref), channel_id=1, source_target_pairs={{1,2},{2,1},{3,4},{4,3},{5,6},{6,5},{7,8},{8,7},{9,10},{10,9},{11,... | collective-permute-start | bytes 196616 | tf_op jit(solution)/shard_map/ppermute | solution.py:324
  47.0 4.7 %collective-permute-done.16.outer_ref = bf16[256,128]{1,0:T(8,128)(2,1)S(1)} collective-permute-done((bf16[256,128]{1,0:T(8,128)(2,1)S(1)}, bf16[256,128]{1,0:T(8,128)(2,1)S(1)}, u32[]{:S(2)}, u32[]{:S(2)}) %collective-permute-start.16) | collective-permute-done | bytes 65568 | tf_op jit(solution)/shard_map/ppermute | solution.py:324
  51.7 0.9 %refine.1 = bf16[256,128]{1,0:T(8,128)(2,1)} custom-call(bf16[256,128]{1,0:T(8,128)(2,1)S(1)} %collective-permute-done.16.outer_ref, bf16[256,128]{1,0:T(8,128)(2,1)S(1)} %merge.1.here_ref, f32[256,384]{1,0:T(8,128)S(1)} %near_rows.1.near_ref, bf16[3,3,128,128]{3,2,1,0:T(8,128)(2,1)S(1)} %copy-done), custom_call_target="tpu_custom_call" | custom-call | tf_op jit(solution)/shard_map/refine/pallas_call | solution.py:283
  (37 shorter events, 3.9 us)
Async XLA Ops:
  0.0 6.0 %collective-permute-start = (bf16[256,128]{1,0:T(8,128)(2,1)}, bf16[256,128]{1,0:T(8,128)(2,1)S(1)}, u32[]{:S(2)}, u32[]{:S(2)}) collective-permute-start(bf16[256,128]{1,0:T(8,128)(2,1)} %own_ref.1), channel_id=1, source_target_pairs={{0,32},{1,65},{2,34},{3,67},{4,36},{5,69},{6,38},{7,71},{8,40},{9,... | collective-permute-start | bytes 196616 | tf_op jit(solution)/shard_map/ppermute | solution.py:44
  3.0 4.5 %collective-permute-start.1 = (bf16[256,128]{1,0:T(8,128)(2,1)}, bf16[256,128]{1,0:T(8,128)(2,1)S(1)}, u32[]{:S(2)}, u32[]{:S(2)}) collective-permute-start(bf16[256,128]{1,0:T(8,128)(2,1)} %own_ref.1), channel_id=1, source_target_pairs={{0,16},{1,9},{2,18},{3,11},{4,20},{5,13},{6,22},{7,15},{8,24},{9,1... | collective-permute-start | bytes 196616 | tf_op jit(solution)/shard_map/ppermute | solution.py:44
  3.6 5.7 %collective-permute-start.2 = (bf16[256,128]{1,0:T(8,128)(2,1)}, bf16[256,128]{1,0:T(8,128)(2,1)S(1)}, u32[]{:S(2)}, u32[]{:S(2)}) collective-permute-start(bf16[256,128]{1,0:T(8,128)(2,1)} %own_ref.1), channel_id=1, source_target_pairs={{0,48},{1,73},{2,50},{3,75},{4,52},{5,77},{6,54},{7,79},{8,56},{9,... | collective-permute-start | bytes 196616 | tf_op jit(solution)/shard_map/ppermute | solution.py:44
  4.2 0.9 %copy-start.1 = (bf16[256,128]{1,0:T(8,128)(2,1)S(1)}, bf16[256,128]{1,0:T(8,128)(2,1)}, u32[]{:S(2)}) copy-start(bf16[256,128]{1,0:T(8,128)(2,1)} %own_ref.1) | copy-start | bytes 196612
  5.0 4.4 %copy-start.2 = (bf16[256,128]{1,0:T(8,128)(2,1)S(1)}, bf16[256,128]{1,0:T(8,128)(2,1)}, u32[]{:S(2)}) copy-start(bf16[256,128]{1,0:T(8,128)(2,1)} %q_ref.1) | copy-start | bytes 196612
  9.3 14.6 %collective-permute-start.8 = (bf16[1024,128]{1,0:T(8,128)(2,1)S(1)}, bf16[1024,128]{1,0:T(8,128)(2,1)S(1)}, u32[]{:S(2)}, u32[]{:S(2)}) collective-permute-start(bf16[1024,128]{1,0:T(8,128)(2,1)S(1)} %join.1.refs_4_), channel_id=1, source_target_pairs={{0,1},{1,0},{2,3},{3,2},{4,5},{5,4},{6,7},{7,6},{8,9},{9,8},{10,11... | collective-permute-start | bytes 786440 | tf_op jit(solution)/shard_map/ppermute | solution.py:48
  9.4 5.8 %collective-permute-start.6 = (bf16[256,128]{1,0:T(8,128)(2,1)S(1)}, bf16[256,128]{1,0:T(8,128)(2,1)S(1)}, u32[]{:S(2)}, u32[]{:S(2)}) collective-permute-start(bf16[256,128]{1,0:T(8,128)(2,1)S(1)} %copy-done.2), channel_id=1, source_target_pairs={{0,6},{1,7},{2,4},{3,5},{4,2},{5,3},{6,0},{7,1},{8,14},{9,15},{10,... | collective-permute-start | bytes 196616 | tf_op jit(solution)/shard_map/ppermute | solution.py:44
  12.5 13.1 %collective-permute-start.3 = (bf16[1024,128]{1,0:T(8,128)(2,1)S(1)}, bf16[1024,128]{1,0:T(8,128)(2,1)S(1)}, u32[]{:S(2)}, u32[]{:S(2)}) collective-permute-start(bf16[1024,128]{1,0:T(8,128)(2,1)S(1)} %join.1.refs_4_), channel_id=1, source_target_pairs={{0,8},{1,17},{2,10},{3,19},{4,12},{5,21},{6,14},{7,23},{8,0},{9,25... | collective-permute-start | bytes 786440 | tf_op jit(solution)/shard_map/ppermute | solution.py:44
  14.1 11.4 %collective-permute-start.4 = (bf16[1024,128]{1,0:T(8,128)(2,1)S(1)}, bf16[1024,128]{1,0:T(8,128)(2,1)S(1)}, u32[]{:S(2)}, u32[]{:S(2)}) collective-permute-start(bf16[1024,128]{1,0:T(8,128)(2,1)S(1)} %join.1.refs_4_), channel_id=1, source_target_pairs={{0,72},{1,49},{2,74},{3,51},{4,76},{5,53},{6,78},{7,55},{8,64},{9,... | collective-permute-start | bytes 786440 | tf_op jit(solution)/shard_map/ppermute | solution.py:44
  14.1 6.0 %collective-permute-start.7 = (bf16[256,128]{1,0:T(8,128)(2,1)S(1)}, bf16[256,128]{1,0:T(8,128)(2,1)S(1)}, u32[]{:S(2)}, u32[]{:S(2)}) collective-permute-start(bf16[256,128]{1,0:T(8,128)(2,1)S(1)} %copy-done.2), channel_id=1, source_target_pairs={{0,4},{1,5},{2,6},{3,7},{4,0},{5,1},{6,2},{7,3},{8,12},{9,13},{10,... | collective-permute-start | bytes 196616 | tf_op jit(solution)/shard_map/ppermute | solution.py:44
  15.2 7.2 %collective-permute-start.5 = (bf16[256,128]{1,0:T(8,128)(2,1)S(1)}, bf16[256,128]{1,0:T(8,128)(2,1)S(1)}, u32[]{:S(2)}, u32[]{:S(2)}) collective-permute-start(bf16[256,128]{1,0:T(8,128)(2,1)S(1)} %copy-done.2), channel_id=1, source_target_pairs={{0,2},{1,3},{2,0},{3,1},{4,6},{5,7},{6,4},{7,5},{8,10},{9,11},{10,... | collective-permute-start | bytes 196616 | tf_op jit(solution)/shard_map/ppermute | solution.py:44
  20.1 8.3 %collective-permute-start.11 = (bf16[1024,128]{1,0:T(8,128)(2,1)S(1)}, bf16[1024,128]{1,0:T(8,128)(2,1)S(1)}, u32[]{:S(2)}, u32[]{:S(2)}) collective-permute-start(bf16[1024,128]{1,0:T(8,128)(2,1)S(1)} %join.1.refs_4_), channel_id=1, source_target_pairs={{0,64},{1,33},{2,66},{3,35},{4,68},{5,37},{6,70},{7,39},{8,72},{9,... | collective-permute-start | bytes 786440 | tf_op jit(solution)/shard_map/ppermute | solution.py:44
  25.6 3.0 %collective-permute-start.10 = (bf16[1024,128]{1,0:T(8,128)(2,1)S(1)}, bf16[1024,128]{1,0:T(8,128)(2,1)S(1)}, u32[]{:S(2)}, u32[]{:S(2)}) collective-permute-start(bf16[1024,128]{1,0:T(8,128)(2,1)S(1)} %collective-permute-done.4.refs_4_), channel_id=1, source_target_pairs={{0,1},{1,0},{2,3},{3,2},{4,5},{5,4},{6,7},{7,6},{8,9},{9,8},{10,11... | collective-permute-start | bytes 786440 | tf_op jit(solution)/shard_map/ppermute | solution.py:48
  25.7 2.9 %collective-permute-start.9 = (bf16[1024,128]{1,0:T(8,128)(2,1)S(1)}, bf16[1024,128]{1,0:T(8,128)(2,1)S(1)}, u32[]{:S(2)}, u32[]{:S(2)}) collective-permute-start(bf16[1024,128]{1,0:T(8,128)(2,1)S(1)} %collective-permute-done.3.refs_3_), channel_id=1, source_target_pairs={{0,1},{1,0},{2,3},{3,2},{4,5},{5,4},{6,7},{7,6},{8,9},{9,8},{10,11... | collective-permute-start | bytes 786440 | tf_op jit(solution)/shard_map/ppermute | solution.py:48
  28.4 1.8 %collective-permute-start.12 = (bf16[1024,128]{1,0:T(8,128)(2,1)S(1)}, bf16[1024,128]{1,0:T(8,128)(2,1)S(1)}, u32[]{:S(2)}, u32[]{:S(2)}) collective-permute-start(bf16[1024,128]{1,0:T(8,128)(2,1)S(1)} %collective-permute-done.11.refs_7_.refs_3_.refs_5_), channel_id=1, source_target_pairs={{0,1},{1,0},{2,3},{3,2},{4,5},{5,4},{6,7},{7,6},{8,9},{9,8},{10,11... | collective-permute-start | bytes 786440 | tf_op jit(solution)/shard_map/ppermute | solution.py:48
  31.8 8.7 %collective-permute-start.15 = (bf16[272,128]{1,0:T(8,128)(2,1)S(1)}, bf16[272,128]{1,0:T(8,128)(2,1)S(1)}, u32[]{:S(2)}, u32[]{:S(2)}) collective-permute-start(bf16[272,128]{1,0:T(8,128)(2,1)S(1)} %last_keys.7), channel_id=1, source_target_pairs={{0,2},{1,3},{2,0},{3,1},{4,6},{5,7},{6,4},{7,5},{8,10},{9,11},{10,... | collective-permute-start | bytes 208904 | tf_op jit(solution)/shard_map/ppermute | solution.py:44
  33.2 7.3 %collective-permute-start.14 = (bf16[272,128]{1,0:T(8,128)(2,1)S(1)}, bf16[272,128]{1,0:T(8,128)(2,1)S(1)}, u32[]{:S(2)}, u32[]{:S(2)}) collective-permute-start(bf16[272,128]{1,0:T(8,128)(2,1)S(1)} %last_keys.6), channel_id=1, source_target_pairs={{0,6},{1,7},{2,4},{3,5},{4,2},{5,3},{6,0},{7,1},{8,14},{9,15},{10,... | collective-permute-start | bytes 208904 | tf_op jit(solution)/shard_map/ppermute | solution.py:44
  35.4 5.9 %copy-start.3 = (bf16[128,128]{1,0:T(8,128)(2,1)S(1)}, bf16[128,128]{1,0:T(8,128)(2,1)}, u32[]{:S(2)}) copy-start(bf16[128,128]{1,0:T(8,128)(2,1)} %vw_ref.1) | copy-start | bytes 98308
  35.4 5.9 %copy-start.4 = (bf16[128,128]{1,0:T(8,128)(2,1)S(1)}, bf16[128,128]{1,0:T(8,128)(2,1)}, u32[]{:S(2)}) copy-start(bf16[128,128]{1,0:T(8,128)(2,1)} %ow_ref.1) | copy-start | bytes 98308
  35.4 5.9 %collective-permute-start.13 = (bf16[272,128]{1,0:T(8,128)(2,1)S(1)}, bf16[272,128]{1,0:T(8,128)(2,1)S(1)}, u32[]{:S(2)}, u32[]{:S(2)}) collective-permute-start(bf16[272,128]{1,0:T(8,128)(2,1)S(1)} %last_keys.5), channel_id=1, source_target_pairs={{0,4},{1,5},{2,6},{3,7},{4,0},{5,1},{6,2},{7,3},{8,12},{9,13},{10,... | collective-permute-start | bytes 208904 | tf_op jit(solution)/shard_map/ppermute | solution.py:44
  41.3 5.4 %copy-start = (bf16[3,3,128,128]{3,2,1,0:T(8,128)(2,1)S(1)}, bf16[3,3,128,128]{3,2,1,0:T(8,128)(2,1)}, u32[]{:S(2)}) copy-start(bf16[3,3,128,128]{3,2,1,0:T(8,128)(2,1)} %w_ref.3) | copy-start | bytes 884740
  41.8 5.0 %copy-start.5 = (bf16[128]{0:T(256)(128)(2,1)S(1)}, bf16[128]{0:T(256)(128)(2,1)}, u32[]{:S(2)}) copy-start(bf16[128]{0:T(256)(128)(2,1)} %param.11) | copy-start | bytes 772
  41.8 4.9 %collective-permute-start.17 = (bf16[256,128]{1,0:T(8,128)(2,1)S(1)}, bf16[256,128]{1,0:T(8,128)(2,1)S(1)}, u32[]{:S(2)}, u32[]{:S(2)}) collective-permute-start(bf16[256,128]{1,0:T(8,128)(2,1)S(1)} %merge.1.here_ref), channel_id=1, source_target_pairs={{0,1},{1,0},{2,3},{3,2},{4,5},{5,4},{6,7},{7,6},{8,9},{9,8},{10,11... | collective-permute-start | bytes 196616 | tf_op jit(solution)/shard_map/ppermute | solution.py:48
  41.9 9.8 %collective-permute-start.16 = (bf16[256,128]{1,0:T(8,128)(2,1)S(1)}, bf16[256,128]{1,0:T(8,128)(2,1)S(1)}, u32[]{:S(2)}, u32[]{:S(2)}) collective-permute-start(bf16[256,128]{1,0:T(8,128)(2,1)S(1)} %merge.1.here_ref), channel_id=1, source_target_pairs={{1,2},{2,1},{3,4},{4,3},{5,6},{6,5},{7,8},{8,7},{9,10},{10,9},{11,... | collective-permute-start | bytes 196616 | tf_op jit(solution)/shard_map/ppermute | solution.py:324

commit v4 on v3

--- a/solution.py
+++ b/solution.py
@@ -114,38 +114,38 @@
     )(*queries, *pieces, *state)
 
 
-def stage_kernel(own_ref, out_ref):
-    out_ref[0 : own_ref.shape[0]] = own_ref[...]
-
-
-def join_kernel(staged_ref, *refs):
-    out_ref = refs[-1]
-    for i, ref in enumerate(refs[:-1]):
+def pause_kernel(out_ref):
+    out_ref[...] = jnp.zeros_like(out_ref)
+
+
+def pause_call():
+    return pl.pallas_call(
+        pause_kernel,
+        out_shape=jax.ShapeDtypeStruct((8, 128), jnp.float32),
+        out_specs=VMEM,
+        compiler_params=params(),
+        cost_estimate=pl.CostEstimate(flops=20_000_000_000, transcendentals=0, bytes_accessed=4096),
+        name="pause",
+    )()
+
+
+def join_kernel(*refs):
+    blocks, out_ref = refs[:-2], refs[-1]
+    for i, ref in enumerate(blocks):
         rows = ref.shape[0]
-        out_ref[(i + 1) * rows : (i + 2) * rows] = ref[...]
-
-
-def stage_call(own, count):
-    return pl.pallas_call(
-        stage_kernel,
-        out_shape=jax.ShapeDtypeStruct((own.shape[0] * count, 128), own.dtype),
-        in_specs=[VMEM],
-        out_specs=VMEM,
-        compiler_params=params(),
-        name="stage",
-    )(own)
-
-
-def join_call(staged, blocks):
+        out_ref[i * rows : (i + 1) * rows] = ref[...]
+
+
+def join_call(blocks, after):
+    rows = sum(block.shape[0] for block in blocks)
     return pl.pallas_call(
         join_kernel,
-        out_shape=jax.ShapeDtypeStruct(staged.shape, staged.dtype),
-        in_specs=[VMEM] * (1 + len(blocks)),
-        out_specs=VMEM,
-        input_output_aliases={0: 0},
+        out_shape=jax.ShapeDtypeStruct((rows, 128), blocks[0].dtype),
+        in_specs=[VMEM] * (len(blocks) + 1),
+        out_specs=VMEM,
         compiler_params=params(),
         name="join",
-    )(staged, *blocks)
+    )(*blocks, after)
 
 
 def split3(x):
@@ -295,7 +295,7 @@
     fence = lax.optimization_barrier
     near = [trade(feat_second, kind, "x", "z") for kind in ("AB", "A", "B")]
     queries = [trade(feat_first, kind, "y") for kind in ("AB", "A", "B")]
-    mine = join_call(stage_call(feat_second, 4), near)
+    mine = join_call([feat_second] + near, pause_call())
     far_a, far_b, far_ab = [trade(mine, kind, "z", "x") for kind in ("A", "B", "AB")]
     twin = swap(mine)
     query_ab, query_a, query_b = queries

time: 52.7 us -> 52.7 us (level)
  local copies, waits for them, and re-layouts: 0.89 us -> 0.02 us
  waiting for transfers between devices: 14.7 us -> 15.5 us
    ppermute x12, waiting for transfers between devices: 10 us -> 10.9 us  [trade(): return lax.ppermute(block, AXES, pairs)]
    unnamed x12, local copies, waits for them, and re-layouts: 0.89 us -> 0.02 us
where the time goes in v4:
time: 52.7 us; the launch traced here: 52.6 us
  starting transfers between devices  22.3 us (42%)
  waiting for transfers between devices  15.5 us (29%)
  Pallas kernels  14.5 us (28%)
    ppermute x12, starting transfers between devices, trade(): return lax.ppermute(block, AXES, pairs)  16.5 us
    ppermute x12, waiting for transfers between devices, trade(): return lax.ppermute(block, AXES, pairs)  10.9 us
    pallas_call x4, Pallas kernels, keys_call(): pl.pallas_call(functools.partial(keys_kernel, scale, len(queries), len(pi...  6.95 us
    pallas_call x4, Pallas kernels, last_call(): pl.pallas_call(functools.partial(last_kernel, scale, row, len(pieces), pa...  5.9 us
    ppermute x1, starting transfers between devices, local(): lax.ppermute(mixed, AXES, [(i, i + 1 if i % 2 else i - 1) for i in range(...  4.84 us
    ppermute x1, waiting for transfers between devices, local(): lax.ppermute(mixed, AXES, [(i, i + 1 if i % 2 else i - 1) for i in range(...  4.65 us
  transfers between devices with their start and end apart: 18, of which 7 were waited for; matrix products, arithmetic and copies ran while one was open for 0% of the time, Pallas kernels for 22%

profile of v4, /device:TPU:64, one launch (start us, length us, event | category | flops | bytes accessed | tf_op | source)
XLA Modules:
  0.0 52.6 jit_solution(8644633180372139909)
XLA Ops:
  0.0 3.0 %collective-permute-start = (bf16[256,128]{1,0:T(8,128)(2,1)}, bf16[256,128]{1,0:T(8,128)(2,1)S(1)}, u32[]{:S(2)}, u32[]{:S(2)}) collective-permute-start(bf16[256,128]{1,0:T(8,128)(2,1)} %refs_0_.4), channel_id=1, source_target_pairs={{0,32},{1,65},{2,34},{3,67},{4,36},{5,69},{6,38},{7,71},{8,40},{9,... | collective-permute-start | bytes 196616 | tf_op jit(solution)/shard_map/ppermute | solution.py:44
  3.0 0.6 %collective-permute-start.1 = (bf16[256,128]{1,0:T(8,128)(2,1)}, bf16[256,128]{1,0:T(8,128)(2,1)S(1)}, u32[]{:S(2)}, u32[]{:S(2)}) collective-permute-start(bf16[256,128]{1,0:T(8,128)(2,1)} %refs_0_.4), channel_id=1, source_target_pairs={{0,16},{1,9},{2,18},{3,11},{4,20},{5,13},{6,22},{7,15},{8,24},{9,1... | collective-permute-start | bytes 196616 | tf_op jit(solution)/shard_map/ppermute | solution.py:44
  4.2 1.8 %collective-permute-done.refs_1_ = bf16[256,128]{1,0:T(8,128)(2,1)S(1)} collective-permute-done((bf16[256,128]{1,0:T(8,128)(2,1)}, bf16[256,128]{1,0:T(8,128)(2,1)S(1)}, u32[]{:S(2)}, u32[]{:S(2)}) %collective-permute-start) | collective-permute-done | bytes 65568 | tf_op jit(solution)/shard_map/ppermute | solution.py:44
  6.0 1.5 %collective-permute-done.1.refs_2_ = bf16[256,128]{1,0:T(8,128)(2,1)S(1)} collective-permute-done((bf16[256,128]{1,0:T(8,128)(2,1)}, bf16[256,128]{1,0:T(8,128)(2,1)S(1)}, u32[]{:S(2)}, u32[]{:S(2)}) %collective-permute-start.1) | collective-permute-done | bytes 65568 | tf_op jit(solution)/shard_map/ppermute | solution.py:44
  7.5 1.8 %collective-permute-done.2.refs_3_ = bf16[256,128]{1,0:T(8,128)(2,1)S(1)} collective-permute-done((bf16[256,128]{1,0:T(8,128)(2,1)}, bf16[256,128]{1,0:T(8,128)(2,1)S(1)}, u32[]{:S(2)}, u32[]{:S(2)}) %collective-permute-start.2) | collective-permute-done | bytes 65568 | tf_op jit(solution)/shard_map/ppermute | solution.py:44
  9.4 3.1 %collective-permute-start.6 = (bf16[256,128]{1,0:T(8,128)(2,1)S(1)}, bf16[256,128]{1,0:T(8,128)(2,1)S(1)}, u32[]{:S(2)}, u32[]{:S(2)}) collective-permute-start(bf16[256,128]{1,0:T(8,128)(2,1)S(1)} %copy-done.1), channel_id=1, source_target_pairs={{0,6},{1,7},{2,4},{3,5},{4,2},{5,3},{6,0},{7,1},{8,14},{9,15},{10,... | collective-permute-start | bytes 196616 | tf_op jit(solution)/shard_map/ppermute | solution.py:44
  12.5 1.6 %collective-permute-start.3 = (bf16[1024,128]{1,0:T(8,128)(2,1)S(1)}, bf16[1024,128]{1,0:T(8,128)(2,1)S(1)}, u32[]{:S(2)}, u32[]{:S(2)}) collective-permute-start(bf16[1024,128]{1,0:T(8,128)(2,1)S(1)} %join.1.refs_4_), channel_id=1, source_target_pairs={{0,8},{1,17},{2,10},{3,19},{4,12},{5,21},{6,14},{7,23},{8,0},{9,25... | collective-permute-start | bytes 786440 | tf_op jit(solution)/shard_map/ppermute | solution.py:44
  14.2 0.6 %collective-permute-start.7 = (bf16[256,128]{1,0:T(8,128)(2,1)S(1)}, bf16[256,128]{1,0:T(8,128)(2,1)S(1)}, u32[]{:S(2)}, u32[]{:S(2)}) collective-permute-start(bf16[256,128]{1,0:T(8,128)(2,1)S(1)} %copy-done.1), channel_id=1, source_target_pairs={{0,4},{1,5},{2,6},{3,7},{4,0},{5,1},{6,2},{7,3},{8,12},{9,13},{10,... | collective-permute-start | bytes 196616 | tf_op jit(solution)/shard_map/ppermute | solution.py:44
  15.5 4.6 %collective-permute-done.7.refs_3_.refs_2_.refs_1_.refs_0_ = bf16[256,128]{1,0:T(8,128)(2,1)S(1)} collective-permute-done((bf16[256,128]{1,0:T(8,128)(2,1)S(1)}, bf16[256,128]{1,0:T(8,128)(2,1)S(1)}, u32[]{:S(2)}, u32[]{:S(2)}) %collective-permute-start.7) | collective-permute-done | bytes 65568 | tf_op jit(solution)/shard_map/ppermute | solution.py:44
  20.1 2.3 %collective-permute-start.11 = (bf16[1024,128]{1,0:T(8,128)(2,1)S(1)}, bf16[1024,128]{1,0:T(8,128)(2,1)S(1)}, u32[]{:S(2)}, u32[]{:S(2)}) collective-permute-start(bf16[1024,128]{1,0:T(8,128)(2,1)S(1)} %join.1.refs_4_), channel_id=1, source_target_pairs={{0,64},{1,33},{2,66},{3,35},{4,68},{5,37},{6,70},{7,39},{8,72},{9,... | collective-permute-start | bytes 786440 | tf_op jit(solution)/shard_map/ppermute | solution.py:44
  22.4 1.6 %keys.4 = (f32[1024,128]{1,0:T(8,128)S(1)}, f32[1024,256]{1,0:T(8,128)S(1)}) custom-call(bf16[256,128]{1,0:T(8,128)(2,1)S(1)} %copy-done.1, bf16[256,128]{1,0:T(8,128)(2,1)S(1)} %collective-permute-done.5.refs_1_.refs_0_, bf16[256,128]{1,0:T(8,128)(2,1)S(1)} %collective-permute-done.6.refs_2_.refs_1_.refs_0_, ...), custom_call_target="tpu_custom_call" | custom-call | flops 805306368 | bytes 1048576 | tf_op jit(solution)/shard_map/keys/pallas_call | solution.py:103
  24.0 1.6 %keys.5 = (f32[1024,128]{1,0:T(8,128)S(1)}, f32[1024,256]{1,0:T(8,128)S(1)}) custom-call(bf16[256,128]{1,0:T(8,128)(2,1)S(1)} %copy-done.1, bf16[256,128]{1,0:T(8,128)(2,1)S(1)} %collective-permute-done.5.refs_1_.refs_0_, bf16[256,128]{1,0:T(8,128)(2,1)S(1)} %collective-permute-done.6.refs_2_.refs_1_.refs_0_, ...), custom_call_target="tpu_custom_call" | custom-call | flops 805306368 | bytes 1048576 | tf_op jit(solution)/shard_map/keys/pallas_call | solution.py:103
  26.2 2.2 %keys.6 = (f32[768,128]{1,0:T(8,128)S(1)}, f32[768,256]{1,0:T(8,128)S(1)}) custom-call(bf16[256,128]{1,0:T(8,128)(2,1)S(1)} %collective-permute-done.5.refs_1_.refs_0_, bf16[256,128]{1,0:T(8,128)(2,1)S(1)} %collective-permute-done.6.refs_2_.refs_1_.refs_0_, bf16[256,128]{1,0:T(8,128)(2,1)S(1)} %collective-permute-done.7.refs_3_.refs_2_.refs_1_.refs_0_, ...), custom_call_target="tpu_custom_call" | custom-call | flops 1207959552 | bytes 1048576 | tf_op jit(solution)/shard_map/keys/pallas_call | solution.py:103
  28.6 1.6 %keys.7 = (f32[512,128]{1,0:T(8,128)S(1)}, f32[512,256]{1,0:T(8,128)S(1)}) custom-call(bf16[256,128]{1,0:T(8,128)(2,1)S(1)} %collective-permute-done.6.refs_2_.refs_1_.refs_0_, bf16[256,128]{1,0:T(8,128)(2,1)S(1)} %collective-permute-done.7.refs_3_.refs_2_.refs_1_.refs_0_, bf16[1024,128]{1,0:T(8,128)(2,1)S(1)} %collective-permute-done.9.refs_2_.refs_5_.refs_3_, ...), custom_call_target="tpu_custom_call" | custom-call | flops 805306368 | bytes 1048576 | tf_op jit(solution)/shard_map/keys/pallas_call | solution.py:103
  30.2 1.6 %last_keys.7 = bf16[272,128]{1,0:T(8,128)(2,1)S(1)} custom-call(bf16[256,128]{1,0:T(8,128)(2,1)S(1)} %collective-permute-done.5.refs_1_.refs_0_, f32[768,128]{1,0:T(8,128)S(1)} %get-tuple-element.42.refs_4_.refs_1_, f32[768,256]{1,0:T(8,128)S(1)} %get-tuple-element.43.refs_5_.refs_2_, bf16[1024,128]{1,0:T(8,128)(2,1)S(1)} %collective-permute-done.9.refs_2_.refs_5_.refs_3_, ...), custom_call_target="tpu_custom_call" | custom-call | flops 805306368 | bytes 1048576 | tf_op jit(solution)/shard_map/last_keys/pallas_call | solution.py:213
  32.2 1.0 %last_keys.6 = bf16[272,128]{1,0:T(8,128)(2,1)S(1)} custom-call(bf16[256,128]{1,0:T(8,128)(2,1)S(1)} %collective-permute-done.6.refs_2_.refs_1_.refs_0_, f32[512,128]{1,0:T(8,128)S(1)} %get-tuple-element.49.refs_1_, f32[512,256]{1,0:T(8,128)S(1)} %get-tuple-element.50.refs_2_, bf16[1024,128]{1,0:T(8,128)(2,1)S(1)} %collective-permute-done.11.refs_7_.refs_3_.refs_5_, ...), custom_call_target="tpu_custom_call" | custom-call | flops 402653184 | bytes 1048576 | tf_op jit(solution)/shard_map/last_keys/pallas_call | solution.py:213
  33.3 1.1 %collective-permute-start.14 = (bf16[272,128]{1,0:T(8,128)(2,1)S(1)}, bf16[272,128]{1,0:T(8,128)(2,1)S(1)}, u32[]{:S(2)}, u32[]{:S(2)}) collective-permute-start(bf16[272,128]{1,0:T(8,128)(2,1)S(1)} %last_keys.6), channel_id=1, source_target_pairs={{0,6},{1,7},{2,4},{3,5},{4,2},{5,3},{6,0},{7,1},{8,14},{9,15},{10,... | collective-permute-start | bytes 208904 | tf_op jit(solution)/shard_map/ppermute | solution.py:44
  34.4 1.0 %last_keys.5 = bf16[272,128]{1,0:T(8,128)(2,1)S(1)} custom-call(bf16[256,128]{1,0:T(8,128)(2,1)S(1)} %collective-permute-done.7.refs_3_.refs_2_.refs_1_.refs_0_, f32[512,128]{1,0:T(8,128)S(1)} %get-tuple-element.49.refs_1_, f32[512,256]{1,0:T(8,128)S(1)} %get-tuple-element.50.refs_2_, bf16[1024,128]{1,0:T(8,128)(2,1)S(1)} %collective-permute-done.11.refs_7_.refs_3_.refs_5_, ...), custom_call_target="tpu_custom_call" | custom-call | flops 402653184 | bytes 1048576 | tf_op jit(solution)/shard_map/last_keys/pallas_call | solution.py:213
  35.4 3.0 %collective-permute-start.13 = (bf16[272,128]{1,0:T(8,128)(2,1)S(1)}, bf16[272,128]{1,0:T(8,128)(2,1)S(1)}, u32[]{:S(2)}, u32[]{:S(2)}) collective-permute-start(bf16[272,128]{1,0:T(8,128)(2,1)S(1)} %last_keys.5), channel_id=1, source_target_pairs={{0,4},{1,5},{2,6},{3,7},{4,0},{5,1},{6,2},{7,3},{8,12},{9,13},{10,... | collective-permute-start | bytes 208904 | tf_op jit(solution)/shard_map/ppermute | solution.py:44
  38.4 2.2 %last_keys.4 = (f32[256,128]{1,0:T(8,128)S(1)}, f32[256,256]{1,0:T(8,128)S(1)}) custom-call(bf16[256,128]{1,0:T(8,128)(2,1)S(1)} %copy-done.1, f32[1024,128]{1,0:T(8,128)S(1)} %get-tuple-element.35.refs_5_.refs_1_, f32[1024,256]{1,0:T(8,128)S(1)} %get-tuple-element.36.refs_6_.refs_2_, bf16[1024,128]{1,0:T(8,128)(2,1)S(1)} %collective-permute-done.3.refs_3_, ...), custom_call_target="tpu_custom_call" | custom-call | flops 1207959552 | bytes 1048576 | tf_op jit(solution)/shard_map/last_keys/pallas_call | solution.py:213
  40.6 0.7 %collective-permute-done.13.refs_0_ = bf16[272,128]{1,0:T(8,128)(2,1)S(1)} collective-permute-done((bf16[272,128]{1,0:T(8,128)(2,1)S(1)}, bf16[272,128]{1,0:T(8,128)(2,1)S(1)}, u32[]{:S(2)}, u32[]{:S(2)}) %collective-permute-start.13) | collective-permute-done | bytes 69664 | tf_op jit(solution)/shard_map/ppermute | solution.py:44
  41.9 4.8 %collective-permute-start.16 = (bf16[256,128]{1,0:T(8,128)(2,1)S(1)}, bf16[256,128]{1,0:T(8,128)(2,1)S(1)}, u32[]{:S(2)}, u32[]{:S(2)}) collective-permute-start(bf16[256,128]{1,0:T(8,128)(2,1)S(1)} %merge.1.here_ref), channel_id=1, source_target_pairs={{1,2},{2,1},{3,4},{4,3},{5,6},{6,5},{7,8},{8,7},{9,10},{10,9},{11,... | collective-permute-start | bytes 196616 | tf_op jit(solution)/shard_map/ppermute | solution.py:324
  47.0 4.7 %collective-permute-done.16.outer_ref = bf16[256,128]{1,0:T(8,128)(2,1)S(1)} collective-permute-done((bf16[256,128]{1,0:T(8,128)(2,1)S(1)}, bf16[256,128]{1,0:T(8,128)(2,1)S(1)}, u32[]{:S(2)}, u32[]{:S(2)}) %collective-permute-start.16) | collective-permute-done | bytes 65568 | tf_op jit(solution)/shard_map/ppermute | solution.py:324
  51.7 0.9 %refine.1 = bf16[256,128]{1,0:T(8,128)(2,1)} custom-call(bf16[256,128]{1,0:T(8,128)(2,1)S(1)} %collective-permute-done.16.outer_ref, bf16[256,128]{1,0:T(8,128)(2,1)S(1)} %merge.1.here_ref, f32[256,384]{1,0:T(8,128)S(1)} %near_rows.1.near_ref, bf16[3,3,128,128]{3,2,1,0:T(8,128)(2,1)S(1)} %copy-done), custom_call_target="tpu_custom_call" | custom-call | tf_op jit(solution)/shard_map/refine/pallas_call | solution.py:283
  (37 shorter events, 3.4 us)
Async XLA Ops:
  0.0 9.3 %copy-start.2 = (bf16[256,128]{1,0:T(8,128)(2,1)S(1)}, bf16[256,128]{1,0:T(8,128)(2,1)}, u32[]{:S(2)}) copy-start(bf16[256,128]{1,0:T(8,128)(2,1)} %refs_0_.4) | copy-start | bytes 196612
  0.0 6.0 %collective-permute-start = (bf16[256,128]{1,0:T(8,128)(2,1)}, bf16[256,128]{1,0:T(8,128)(2,1)S(1)}, u32[]{:S(2)}, u32[]{:S(2)}) collective-permute-start(bf16[256,128]{1,0:T(8,128)(2,1)} %refs_0_.4), channel_id=1, source_target_pairs={{0,32},{1,65},{2,34},{3,67},{4,36},{5,69},{6,38},{7,71},{8,40},{9,... | collective-permute-start | bytes 196616 | tf_op jit(solution)/shard_map/ppermute | solution.py:44
  3.0 4.5 %collective-permute-start.1 = (bf16[256,128]{1,0:T(8,128)(2,1)}, bf16[256,128]{1,0:T(8,128)(2,1)S(1)}, u32[]{:S(2)}, u32[]{:S(2)}) collective-permute-start(bf16[256,128]{1,0:T(8,128)(2,1)} %refs_0_.4), channel_id=1, source_target_pairs={{0,16},{1,9},{2,18},{3,11},{4,20},{5,13},{6,22},{7,15},{8,24},{9,1... | collective-permute-start | bytes 196616 | tf_op jit(solution)/shard_map/ppermute | solution.py:44
  3.6 5.7 %collective-permute-start.2 = (bf16[256,128]{1,0:T(8,128)(2,1)}, bf16[256,128]{1,0:T(8,128)(2,1)S(1)}, u32[]{:S(2)}, u32[]{:S(2)}) collective-permute-start(bf16[256,128]{1,0:T(8,128)(2,1)} %refs_0_.4), channel_id=1, source_target_pairs={{0,48},{1,73},{2,50},{3,75},{4,52},{5,77},{6,54},{7,79},{8,56},{9,... | collective-permute-start | bytes 196616 | tf_op jit(solution)/shard_map/ppermute | solution.py:44
  4.2 5.3 %copy-start.1 = (bf16[256,128]{1,0:T(8,128)(2,1)S(1)}, bf16[256,128]{1,0:T(8,128)(2,1)}, u32[]{:S(2)}) copy-start(bf16[256,128]{1,0:T(8,128)(2,1)} %q_ref.1) | copy-start | bytes 196612
  9.3 14.6 %collective-permute-start.8 = (bf16[1024,128]{1,0:T(8,128)(2,1)S(1)}, bf16[1024,128]{1,0:T(8,128)(2,1)S(1)}, u32[]{:S(2)}, u32[]{:S(2)}) collective-permute-start(bf16[1024,128]{1,0:T(8,128)(2,1)S(1)} %join.1.refs_4_), channel_id=1, source_target_pairs={{0,1},{1,0},{2,3},{3,2},{4,5},{5,4},{6,7},{7,6},{8,9},{9,8},{10,11... | collective-permute-start | bytes 786440 | tf_op jit(solution)/shard_map/ppermute | solution.py:48
  9.4 5.8 %collective-permute-start.6 = (bf16[256,128]{1,0:T(8,128)(2,1)S(1)}, bf16[256,128]{1,0:T(8,128)(2,1)S(1)}, u32[]{:S(2)}, u32[]{:S(2)}) collective-permute-start(bf16[256,128]{1,0:T(8,128)(2,1)S(1)} %copy-done.1), channel_id=1, source_target_pairs={{0,6},{1,7},{2,4},{3,5},{4,2},{5,3},{6,0},{7,1},{8,14},{9,15},{10,... | collective-permute-start | bytes 196616 | tf_op jit(solution)/shard_map/ppermute | solution.py:44
  12.5 13.1 %collective-permute-start.3 = (bf16[1024,128]{1,0:T(8,128)(2,1)S(1)}, bf16[1024,128]{1,0:T(8,128)(2,1)S(1)}, u32[]{:S(2)}, u32[]{:S(2)}) collective-permute-start(bf16[1024,128]{1,0:T(8,128)(2,1)S(1)} %join.1.refs_4_), channel_id=1, source_target_pairs={{0,8},{1,17},{2,10},{3,19},{4,12},{5,21},{6,14},{7,23},{8,0},{9,25... | collective-permute-start | bytes 786440 | tf_op jit(solution)/shard_map/ppermute | solution.py:44
  14.2 11.4 %collective-permute-start.4 = (bf16[1024,128]{1,0:T(8,128)(2,1)S(1)}, bf16[1024,128]{1,0:T(8,128)(2,1)S(1)}, u32[]{:S(2)}, u32[]{:S(2)}) collective-permute-start(bf16[1024,128]{1,0:T(8,128)(2,1)S(1)} %join.1.refs_4_), channel_id=1, source_target_pairs={{0,72},{1,49},{2,74},{3,51},{4,76},{5,53},{6,78},{7,55},{8,64},{9,... | collective-permute-start | bytes 786440 | tf_op jit(solution)/shard_map/ppermute | solution.py:44
  14.2 6.0 %collective-permute-start.7 = (bf16[256,128]{1,0:T(8,128)(2,1)S(1)}, bf16[256,128]{1,0:T(8,128)(2,1)S(1)}, u32[]{:S(2)}, u32[]{:S(2)}) collective-permute-start(bf16[256,128]{1,0:T(8,128)(2,1)S(1)} %copy-done.1), channel_id=1, source_target_pairs={{0,4},{1,5},{2,6},{3,7},{4,0},{5,1},{6,2},{7,3},{8,12},{9,13},{10,... | collective-permute-start | bytes 196616 | tf_op jit(solution)/shard_map/ppermute | solution.py:44
  15.2 7.2 %collective-permute-start.5 = (bf16[256,128]{1,0:T(8,128)(2,1)S(1)}, bf16[256,128]{1,0:T(8,128)(2,1)S(1)}, u32[]{:S(2)}, u32[]{:S(2)}) collective-permute-start(bf16[256,128]{1,0:T(8,128)(2,1)S(1)} %copy-done.1), channel_id=1, source_target_pairs={{0,2},{1,3},{2,0},{3,1},{4,6},{5,7},{6,4},{7,5},{8,10},{9,11},{10,... | collective-permute-start | bytes 196616 | tf_op jit(solution)/shard_map/ppermute | solution.py:44
  20.1 8.3 %collective-permute-start.11 = (bf16[1024,128]{1,0:T(8,128)(2,1)S(1)}, bf16[1024,128]{1,0:T(8,128)(2,1)S(1)}, u32[]{:S(2)}, u32[]{:S(2)}) collective-permute-start(bf16[1024,128]{1,0:T(8,128)(2,1)S(1)} %join.1.refs_4_), channel_id=1, source_target_pairs={{0,64},{1,33},{2,66},{3,35},{4,68},{5,37},{6,70},{7,39},{8,72},{9,... | collective-permute-start | bytes 786440 | tf_op jit(solution)/shard_map/ppermute | solution.py:44
  25.6 3.0 %collective-permute-start.10 = (bf16[1024,128]{1,0:T(8,128)(2,1)S(1)}, bf16[1024,128]{1,0:T(8,128)(2,1)S(1)}, u32[]{:S(2)}, u32[]{:S(2)}) collective-permute-start(bf16[1024,128]{1,0:T(8,128)(2,1)S(1)} %collective-permute-done.4.refs_4_), channel_id=1, source_target_pairs={{0,1},{1,0},{2,3},{3,2},{4,5},{5,4},{6,7},{7,6},{8,9},{9,8},{10,11... | collective-permute-start | bytes 786440 | tf_op jit(solution)/shard_map/ppermute | solution.py:48
  25.7 2.9 %collective-permute-start.9 = (bf16[1024,128]{1,0:T(8,128)(2,1)S(1)}, bf16[1024,128]{1,0:T(8,128)(2,1)S(1)}, u32[]{:S(2)}, u32[]{:S(2)}) collective-permute-start(bf16[1024,128]{1,0:T(8,128)(2,1)S(1)} %collective-permute-done.3.refs_3_), channel_id=1, source_target_pairs={{0,1},{1,0},{2,3},{3,2},{4,5},{5,4},{6,7},{7,6},{8,9},{9,8},{10,11... | collective-permute-start | bytes 786440 | tf_op jit(solution)/shard_map/ppermute | solution.py:48
  28.4 1.8 %collective-permute-start.12 = (bf16[1024,128]{1,0:T(8,128)(2,1)S(1)}, bf16[1024,128]{1,0:T(8,128)(2,1)S(1)}, u32[]{:S(2)}, u32[]{:S(2)}) collective-permute-start(bf16[1024,128]{1,0:T(8,128)(2,1)S(1)} %collective-permute-done.11.refs_7_.refs_3_.refs_5_), channel_id=1, source_target_pairs={{0,1},{1,0},{2,3},{3,2},{4,5},{5,4},{6,7},{7,6},{8,9},{9,8},{10,11... | collective-permute-start | bytes 786440 | tf_op jit(solution)/shard_map/ppermute | solution.py:48
  31.8 8.7 %collective-permute-start.15 = (bf16[272,128]{1,0:T(8,128)(2,1)S(1)}, bf16[272,128]{1,0:T(8,128)(2,1)S(1)}, u32[]{:S(2)}, u32[]{:S(2)}) collective-permute-start(bf16[272,128]{1,0:T(8,128)(2,1)S(1)} %last_keys.7), channel_id=1, source_target_pairs={{0,2},{1,3},{2,0},{3,1},{4,6},{5,7},{6,4},{7,5},{8,10},{9,11},{10,... | collective-permute-start | bytes 208904 | tf_op jit(solution)/shard_map/ppermute | solution.py:44
  33.3 7.3 %collective-permute-start.14 = (bf16[272,128]{1,0:T(8,128)(2,1)S(1)}, bf16[272,128]{1,0:T(8,128)(2,1)S(1)}, u32[]{:S(2)}, u32[]{:S(2)}) collective-permute-start(bf16[272,128]{1,0:T(8,128)(2,1)S(1)} %last_keys.6), channel_id=1, source_target_pairs={{0,6},{1,7},{2,4},{3,5},{4,2},{5,3},{6,0},{7,1},{8,14},{9,15},{10,... | collective-permute-start | bytes 208904 | tf_op jit(solution)/shard_map/ppermute | solution.py:44
  35.4 5.9 %copy-start.3 = (bf16[128,128]{1,0:T(8,128)(2,1)S(1)}, bf16[128,128]{1,0:T(8,128)(2,1)}, u32[]{:S(2)}) copy-start(bf16[128,128]{1,0:T(8,128)(2,1)} %vw_ref.1) | copy-start | bytes 98308
  35.4 5.9 %copy-start.4 = (bf16[128,128]{1,0:T(8,128)(2,1)S(1)}, bf16[128,128]{1,0:T(8,128)(2,1)}, u32[]{:S(2)}) copy-start(bf16[128,128]{1,0:T(8,128)(2,1)} %ow_ref.1) | copy-start | bytes 98308
  35.4 5.9 %collective-permute-start.13 = (bf16[272,128]{1,0:T(8,128)(2,1)S(1)}, bf16[272,128]{1,0:T(8,128)(2,1)S(1)}, u32[]{:S(2)}, u32[]{:S(2)}) collective-permute-start(bf16[272,128]{1,0:T(8,128)(2,1)S(1)} %last_keys.5), channel_id=1, source_target_pairs={{0,4},{1,5},{2,6},{3,7},{4,0},{5,1},{6,2},{7,3},{8,12},{9,13},{10,... | collective-permute-start | bytes 208904 | tf_op jit(solution)/shard_map/ppermute | solution.py:44
  41.3 5.4 %copy-start = (bf16[3,3,128,128]{3,2,1,0:T(8,128)(2,1)S(1)}, bf16[3,3,128,128]{3,2,1,0:T(8,128)(2,1)}, u32[]{:S(2)}) copy-start(bf16[3,3,128,128]{3,2,1,0:T(8,128)(2,1)} %w_ref.3) | copy-start | bytes 884740
  41.8 5.0 %copy-start.5 = (bf16[128]{0:T(256)(128)(2,1)S(1)}, bf16[128]{0:T(256)(128)(2,1)}, u32[]{:S(2)}) copy-start(bf16[128]{0:T(256)(128)(2,1)} %param.11) | copy-start | bytes 772
  41.8 4.9 %collective-permute-start.17 = (bf16[256,128]{1,0:T(8,128)(2,1)S(1)}, bf16[256,128]{1,0:T(8,128)(2,1)S(1)}, u32[]{:S(2)}, u32[]{:S(2)}) collective-permute-start(bf16[256,128]{1,0:T(8,128)(2,1)S(1)} %merge.1.here_ref), channel_id=1, source_target_pairs={{0,1},{1,0},{2,3},{3,2},{4,5},{5,4},{6,7},{7,6},{8,9},{9,8},{10,11... | collective-permute-start | bytes 196616 | tf_op jit(solution)/shard_map/ppermute | solution.py:48
  41.9 9.8 %collective-permute-start.16 = (bf16[256,128]{1,0:T(8,128)(2,1)S(1)}, bf16[256,128]{1,0:T(8,128)(2,1)S(1)}, u32[]{:S(2)}, u32[]{:S(2)}) collective-permute-start(bf16[256,128]{1,0:T(8,128)(2,1)S(1)} %merge.1.here_ref), channel_id=1, source_target_pairs={{1,2},{2,1},{3,4},{4,3},{5,6},{6,5},{7,8},{8,7},{9,10},{10,9},{11,... | collective-permute-start | bytes 196616 | tf_op jit(solution)/shard_map/ppermute | solution.py:324
